TPU v7x, 128 devices: a whole 4x4x4 slice. The times are simulated.
128 devices in a mesh: expert: 16 (over y, z), replica: 4 (over x), tensor: 2 (over core).
Axes of the slice: x: 4, y: 4, z: 4, core: 2. Of those that a mesh axis runs over, the one named last changes fastest.
Arguments:
- tokens: bfloat16 [8192, 2048], P(('expert', 'replica')), may hold values from -6 to 6
- cotangent: bfloat16 [8192, 2048], P(('expert', 'replica')), may hold values from -6 to 6
- routes: int32 [8192, 8], P(('expert', 'replica')), may hold values from 0 to 63, all different within a row; in each aligned block of 128 rows (0 to 127, 128 to 255, ...) at most 32 rows name the same one
- gates: float32 [8192, 8], P(('expert', 'replica')), may hold values from 0.05 to 1
- gate_weight: bfloat16 [64, 2048, 768], P('expert', None, 'tensor'), may hold values from -0.125 to 0.125
- up_weight: bfloat16 [64, 2048, 768], P('expert', None, 'tensor'), may hold values from -0.125 to 0.125
- down_weight: bfloat16 [64, 768, 2048], P('expert', 'tensor'), may hold values from -0.21875 to 0.21875
Outputs:
- token_grad: bfloat16 [8192, 2048], P(('expert', 'replica'), 'tensor')
- gate_weight_grad: bfloat16 [64, 2048, 768], P(('expert', 'replica'), None, 'tensor')
- up_weight_grad: bfloat16 [64, 2048, 768], P(('expert', 'replica'), None, 'tensor')
- down_weight_grad: bfloat16 [64, 768, 2048], P(('expert', 'replica'), 'tensor')
Inputs may be any that keep to these rules, and one draw needn't show every extreme that they name: `routes`: each row names 8 different experts. Within each aligned block of 128 rows (the rows of one device) no expert is named by more than 32 rows, a bound that some block reaches.
All inputs are finite; a program needn't handle non-finite values.
Results may differ from a plain program's by a relative error of at most 0.0095.
Values may be sent and summed in bfloat16 or wider, within the bound.
A program may use at most 192 MiB of HBM per device.

v0:
```python
import jax
import jax.numpy as jnp
from jax import lax
from jax.sharding import PartitionSpec as P


def body(tokens, cotangent, routes, gates, gate_weight, up_weight, down_weight):
    tok_rows = tokens.shape[0]
    full_width = tokens.shape[1]
    top_count = routes.shape[1]
    exp_local = gate_weight.shape[0]
    axis_experts = lax.axis_size("expert")
    total_experts = exp_local * axis_experts
    capacity = 2 * tok_rows * top_count // total_experts
    chosen = routes.reshape(-1)
    one_hot = (chosen[:, None] == jnp.arange(total_experts, dtype=jnp.int32)[None, :]).astype(
        jnp.int32
    )
    earlier = jnp.cumsum(one_hot, axis=0) - one_hot
    slot_rank = jnp.sum(earlier * one_hot, axis=1)
    position = chosen * capacity + slot_rank
    scaled = (gates[:, :, None] * cotangent[:, None, :].astype(jnp.float32)).astype(jnp.bfloat16)
    copies = jnp.broadcast_to(tokens[:, None, :], (tok_rows, top_count, full_width))
    send_width = copies.shape[2]
    blank_rows = jnp.zeros((total_experts * capacity, send_width), jnp.bfloat16)
    sent_rows = blank_rows.at[position].set(copies.reshape(-1, send_width))
    sent_rows = sent_rows.reshape(axis_experts, exp_local * capacity, send_width)
    sent_cots = blank_rows.at[position].set(scaled.reshape(-1, send_width))
    sent_cots = sent_cots.reshape(axis_experts, exp_local * capacity, send_width)
    rows_in, cots_in = (
        lax.all_to_all(sent_rows, "expert", split_axis=0, concat_axis=0, tiled=True),
        lax.all_to_all(sent_cots, "expert", split_axis=0, concat_axis=0, tiled=True),
    )
    rows_in = rows_in.reshape(1, axis_experts, exp_local, capacity, send_width)
    cots_in = cots_in.reshape(1, axis_experts, exp_local, capacity, send_width)
    gate_pre = jnp.einsum(
        "gsecd,edf->gsecf", rows_in, gate_weight, preferred_element_type=jnp.float32
    )
    up_proj = jnp.einsum("gsecd,edf->gsecf", rows_in, up_weight, preferred_element_type=jnp.float32)
    hidden_grad = jnp.einsum(
        "gsecd,efd->gsecf", cots_in, down_weight, preferred_element_type=jnp.float32
    )
    sig_gate = jax.nn.sigmoid(gate_pre)
    activated = gate_pre * sig_gate
    hidden = (activated * up_proj).astype(jnp.bfloat16)
    gate_grad = (hidden_grad * up_proj * sig_gate * (1.0 + gate_pre * (1.0 - sig_gate))).astype(
        jnp.bfloat16
    )
    up_grad = (hidden_grad * activated).astype(jnp.bfloat16)
    row_grads = (
        jnp.einsum("gsecf,edf->gsecd", gate_grad, gate_weight, preferred_element_type=jnp.float32)
        + jnp.einsum("gsecf,edf->gsecd", up_grad, up_weight, preferred_element_type=jnp.float32)
    ).astype(jnp.bfloat16)
    grad_gate = jnp.einsum(
        "gsecd,gsecf->gedf", rows_in, gate_grad, preferred_element_type=jnp.float32
    ).astype(jnp.bfloat16)
    grad_up = jnp.einsum(
        "gsecd,gsecf->gedf", rows_in, up_grad, preferred_element_type=jnp.float32
    ).astype(jnp.bfloat16)
    grad_down = jnp.einsum(
        "gsecf,gsecd->gefd", hidden, cots_in, preferred_element_type=jnp.float32
    ).astype(jnp.bfloat16)
    rounded = lax.optimization_barrier((grad_gate[0], grad_up[0], grad_down[0]))
    summed = (
        lax.psum_scatter(
            rounded[0].astype(jnp.float32).astype(jnp.bfloat16),
            "replica",
            scatter_dimension=0,
            tiled=True,
        ).astype(jnp.float32),
        lax.psum_scatter(
            rounded[1].astype(jnp.float32).astype(jnp.bfloat16),
            "replica",
            scatter_dimension=0,
            tiled=True,
        ).astype(jnp.float32),
        lax.psum_scatter(
            rounded[2].astype(jnp.float32).astype(jnp.bfloat16),
            "replica",
            scatter_dimension=0,
            tiled=True,
        ).astype(jnp.float32),
    )
    gate_out = summed[0].astype(jnp.bfloat16)
    up_out = summed[1].astype(jnp.bfloat16)
    down_out = summed[2].astype(jnp.bfloat16)
    going_home = row_grads.reshape(axis_experts, exp_local * capacity, full_width)
    returned = lax.all_to_all(going_home, "expert", split_axis=0, concat_axis=0, tiled=True)
    returned = returned.reshape(total_experts * capacity, full_width)
    gathered = returned[position].reshape(tok_rows, top_count, full_width)
    pair_sums = lax.psum_scatter(
        gathered.astype(jnp.float32).astype(jnp.bfloat16), "tensor", scatter_dimension=2, tiled=True
    )
    token_grad = jnp.sum(pair_sums, axis=1, dtype=jnp.float32).astype(jnp.bfloat16)
    return (token_grad, gate_out, up_out, down_out)


def solution(mesh):
    in_specs = (
        P(("expert", "replica"), None),
        P(("expert", "replica"), None),
        P(("expert", "replica"), None),
        P(("expert", "replica"), None),
        P("expert", None, "tensor"),
        P("expert", None, "tensor"),
        P("expert", "tensor", None),
    )
    out_specs = (
        P(("expert", "replica"), "tensor"),
        P(("expert", "replica"), None, "tensor"),
        P(("expert", "replica"), None, "tensor"),
        P(("expert", "replica"), "tensor", None),
    )
    return jax.shard_map(body, mesh=mesh, in_specs=in_specs, out_specs=out_specs, check_vma=False)
```

profile of v0, /device:TPU:11, one launch (start us, length us, event | category | flops | bytes accessed | tf_op | source)
XLA Modules:
  0.0 747.9 jit_solution(6712514855410013204)
XLA Ops:
  7.2 0.0 copy-start
  7.2 0.7 broadcast_multiply_fusion
  7.9 0.8 copy.12
  8.7 0.1 eq.29
  8.8 0.1 eq.25
  8.9 0.1 copy.11
  9.0 0.1 mul.60
  9.1 18.0 %reduce-window.6 = s32[64,8,128]{2,1,0:T(8,128)S(1)} reduce-window(s32[64,8,128]{2,1,0:T(8,128)S(1)} %fusion.48, s32[]{:T(128)} %constant.7.clone.1), window={size=1x1x128 pad=0_0x0_0x127_0}, to_apply=%region_0.0 | reduce-window | flops 8323072 | bytes 524292 | tf_op jit(solution)/shard_map/reduce-window
  27.1 0.1 slice.10
  27.3 0.1 copy.14
  27.5 0.1 copy.15
  27.5 0.1 broadcast_add_fusion
  27.7 0.1 fusion.47
  27.8 0.0 copy-done
  27.8 11.2 %scatter_custom_fusion.1 = bf16[2048,2048]{1,0:T(8,128)(2,1)} fusion(s32[1024]{0:T(1024)S(1)} %bitcast.155, bf16[]{:T(256)} %constant.5.clone.1, bf16[128,2048]{1,0:T(8,128)(2,1)S(1)} %copy-done), kind=kCustom, calls=%fused_computation.26 | custom fusion | bytes 8912898 | tf_op jit(solution)/shard_map/scatter | solution.py:26
  39.0 0.0 copy-start.3
  39.0 0.0 copy-start.2
  39.0 8.3 %all-to-all-start.1 = ((bf16[16,128,2048]{2,1,0:T(8,128)(2,1)}), bf16[16,128,2048]{2,1,0:T(8,128)(2,1)}, u32[]{:S(2)}, u32[]{:S(2)}) async-start(bf16[16,128,2048]{2,1,0:T(8,128)(2,1)} %bitcast.147), calls=%async_computation.1 | async-start | bytes 16777216 | tf_op jit(solution)/shard_map/all_to_all | solution.py:31
  47.3 0.0 copy-done.3
  47.3 0.1 copy.16
  47.4 0.1 mul.62
  47.5 0.0 copy-done.2
  47.5 0.1 convert_element_type.66
  47.6 11.6 %scatter_custom_fusion = bf16[2048,2048]{1,0:T(8,128)(2,1)} fusion(s32[1024]{0:T(1024)S(1)} %bitcast.156, f32[128,2048]{1,0:T(8,128)S(1)} %convert_element_type.66, f32[1024]{0:T(1024)S(1)} %mul.62, bf16[]{:T(256)} %constant.5.clone.1), kind=kCustom, calls=%fused_computation.25 | custom fusion | flops 4194304 | bytes 9441282 | tf_op jit(solution)/shard_map/scatter | solution.py:28
  59.3 90.9 %all-to-all-done.1 = bf16[16,128,2048]{2,1,0:T(8,128)(2,1)} async-done(((bf16[16,128,2048]{2,1,0:T(8,128)(2,1)}), bf16[16,128,2048]{2,1,0:T(8,128)(2,1)}, u32[]{:S(2)}, u32[]{:S(2)}) %all-to-all-start.1) | async-done | bytes 8388640 | tf_op jit(solution)/shard_map/all_to_all | solution.py:31
  150.2 0.0 slice-start
  150.2 52.4 %all-to-all-start = ((bf16[16,128,2048]{2,1,0:T(8,128)(2,1)}), bf16[16,128,2048]{2,1,0:T(8,128)(2,1)}, u32[]{:S(2)}, u32[]{:S(2)}) async-start(bf16[16,128,2048]{2,1,0:T(8,128)(2,1)} %bitcast.146), calls=%async_computation | async-start | bytes 16777216 | tf_op jit(solution)/shard_map/all_to_all | solution.py:32
  202.6 0.0 slice-start.1
  202.6 11.5 %fusion.2 = f32[4,16,32,384]{3,2,1,0:T(8,128)} fusion(bf16[16,4,32,2048]{3,2,1,0:T(8,128)(2,1)} %bitcast.14, bf16[4,2048,384]{2,1,0:T(8,128)(2,1)} %param.11), kind=kOutput, calls=%fused_computation.10 | convolution fusion | flops 3221225472 | bytes 17825792 | tf_op jit(solution)/shard_map/gsecd,edf->gsecf/dot_general | solution.py:36
  214.1 0.0 slice-done
  214.1 0.0 slice-done.1
  214.1 8.6 %fusion.4 = f32[4,16,32,384]{3,2,1,0:T(8,128)} fusion(bf16[16,4,32,2048]{3,2,1,0:T(8,128)(2,1)} %bitcast.14, bf16[4,2048,384]{2,1,0:T(8,128)(2,1)S(1)} %bitcast.151), kind=kOutput, calls=%fused_computation.12 | convolution fusion | flops 3221225472 | bytes 17825792 | tf_op jit(solution)/shard_map/gsecd,edf->gsecf/dot_general | solution.py:39
  222.7 82.3 %all-to-all-done = bf16[16,128,2048]{2,1,0:T(8,128)(2,1)} async-done(((bf16[16,128,2048]{2,1,0:T(8,128)(2,1)}), bf16[16,128,2048]{2,1,0:T(8,128)(2,1)}, u32[]{:S(2)}, u32[]{:S(2)}) %all-to-all-start) | async-done | bytes 8388640 | tf_op jit(solution)/shard_map/all_to_all | solution.py:32
  305.0 13.3 %fusion.39 = (bf16[16,4,32,384]{3,2,0,1:T(8,128)(2,1)S(1)}, bf16[16,4,32,384]{3,2,0,1:T(8,128)(2,1)}) fusion(f32[4,16,32,384]{3,2,1,0:T(8,128)} %fusion.2, f32[4,16,32,384]{3,2,1,0:T(8,128)} %fusion.4, bf16[4,384,2048]{2,1,0:T(8,128)(2,1)} %param.13, bf16[16,4,32,2048]{3,2,1,0:T(8,128)(2,1)} %bitcast.6), kind=kOutput, calls=%fused_computation.48 | convolution fusion | flops 3231449088 | bytes 24117248 | tf_op jit(solution)/shard_map/gsecd,efd->gsecf/dot_general | solution.py:40
  318.3 13.5 %fusion.10 = f32[4,16,32,2048]{3,2,1,0:T(8,128)} fusion(bf16[16,4,32,384]{3,2,0,1:T(8,128)(2,1)} %get-tuple-element.11, bf16[4,2048,384]{2,1,0:T(8,128)(2,1)} %param.11), kind=kOutput, calls=%fused_computation.18 | convolution fusion | flops 3221225472 | bytes 24641536 | tf_op jit(solution)/shard_map/gsecf,edf->gsecd/dot_general | solution.py:51
  331.8 12.1 %fusion = bf16[1,16,4,32,2048]{4,3,1,2,0:T(8,128)(2,1)} fusion(f32[4,16,32,2048]{3,2,1,0:T(8,128)} %fusion.10, bf16[16,4,32,384]{3,2,0,1:T(8,128)(2,1)S(1)} %get-tuple-element.10, bf16[4,2048,384]{2,1,0:T(8,128)(2,1)} %param.12), kind=kOutput, calls=%fused_computation.7 | convolution fusion | flops 3229614080 | bytes 33030144 | tf_op jit(solution)/shard_map/gsecf,edf->gsecd/dot_general | solution.py:52
  344.0 8.3 %copy.20 = bf16[1,16,4,32,2048]{4,3,2,1,0:T(8,128)(2,1)} copy(bf16[1,16,4,32,2048]{4,3,1,2,0:T(8,128)(2,1)} %fusion) | data formatting | bytes 16777216 | tf_op jit(solution)/shard_map/convert_element_type | solution.py:53
  352.2 33.2 %all-to-all-start.2 = ((bf16[16,128,2048]{2,1,0:T(8,128)(2,1)}), bf16[16,128,2048]{2,1,0:T(8,128)(2,1)}, u32[]{:S(2)}, u32[]{:S(2)}) async-start(bf16[16,128,2048]{2,1,0:T(8,128)(2,1)} %bitcast.148), calls=%async_computation.2 | async-start | bytes 16777216 | tf_op jit(solution)/shard_map/all_to_all | solution.py:88
  385.5 0.0 reduce-scatter.5.cloned.1.call-start
  385.5 91.8 %all-to-all-done.2 = bf16[16,128,2048]{2,1,0:T(8,128)(2,1)} async-done(((bf16[16,128,2048]{2,1,0:T(8,128)(2,1)}), bf16[16,128,2048]{2,1,0:T(8,128)(2,1)}, u32[]{:S(2)}, u32[]{:S(2)}) %all-to-all-start.2) | async-done | bytes 8388640 | tf_op jit(solution)/shard_map/all_to_all | solution.py:88
  477.3 13.3 %gather_fusion = bf16[1024,2048]{1,0:T(8,128)(2,1)} fusion(bf16[2048,2048]{1,0:T(8,128)(2,1)} %bitcast.36, s32[1024]{0:T(1024)S(1)} %broadcast_clamp_fusion), kind=kCustom, calls=%fused_computation | custom fusion | bytes 8392704 | tf_op jit(solution)/shard_map/gather | solution.py:90
  490.6 0.0 reduce-scatter.5.cloned.1.call-update
  490.6 0.0 reduce-scatter.7.cloned.1.call-start
  490.7 11.5 %bitcast_convert_fusion = bf16[4,384,2048]{2,1,0:T(8,128)(2,1)} fusion(bf16[16,4,32,2048]{3,2,1,0:T(8,128)(2,1)} %bitcast.6, f32[4,16,32,384]{3,2,1,0:T(8,128)} %fusion.4, f32[4,16,32,384]{3,2,1,0:T(8,128)} %fusion.2), kind=kOutput, calls=%fused_computation.4 | convolution fusion | flops 3229089792 | bytes 20971520 | tf_op jit(solution)/shard_map/gsecf,gsecd->gefd/dot_general | solution.py:60
  502.2 10.6 %bitcast_convert_fusion.1 = bf16[4,2048,384]{2,1,0:T(8,128)(2,1)} fusion(bf16[16,4,32,2048]{3,2,1,0:T(8,128)(2,1)} %bitcast.14, bf16[16,4,32,384]{3,2,0,1:T(8,128)(2,1)S(1)} %get-tuple-element.10), kind=kOutput, calls=%fused_computation.5 | convolution fusion | flops 3224371200 | bytes 16252928 | tf_op jit(solution)/shard_map/gsecd,gsecf->gedf/dot_general | solution.py:57
  512.8 11.6 %bitcast_convert_fusion.2 = bf16[4,2048,384]{2,1,0:T(8,128)(2,1)} fusion(bf16[16,4,32,2048]{3,2,1,0:T(8,128)(2,1)} %bitcast.14, bf16[16,4,32,384]{3,2,0,1:T(8,128)(2,1)} %get-tuple-element.11), kind=kOutput, calls=%fused_computation.6 | convolution fusion | flops 3224371200 | bytes 16252928 | tf_op jit(solution)/shard_map/gsecd,gsecf->gedf/dot_general | solution.py:54
  524.4 0.0 reduce-scatter.7.cloned.1.call-update
  524.4 0.0 copy-start.1
  524.4 0.0 reduce-scatter.9.cloned.1.call-start
  524.5 0.7 reduce-scatter.9.cloned.1.call-update
  525.2 0.0 reduce-scatter.11.cloned.1.call-start
  525.2 0.5 reduce-scatter.11.cloned.1.call-update
  525.8 0.0 reduce-scatter.5.cloned.1.call-done
  525.8 3.7 reduce_sum.25
  529.5 78.1 %reduce-scatter.7.cloned.1.call-done = bf16[1,2048,384]{2,1,0:T(8,128)(2,1)} async-done(((bf16[4,2048,384]{2,1,0:T(8,128)(2,1)}), bf16[1,2048,384]{2,1,0:T(8,128)(2,1)}) %reduce-scatter.7.cloned.1.call-update) | async-done | bytes 1572880 | tf_op jit(solution)/shard_map/reduce_scatter | solution.py:65
  607.6 66.8 %reduce-scatter.9.cloned.1.call-done = bf16[1,2048,384]{2,1,0:T(8,128)(2,1)} async-done(((bf16[4,2048,384]{2,1,0:T(8,128)(2,1)}), bf16[1,2048,384]{2,1,0:T(8,128)(2,1)}) %reduce-scatter.9.cloned.1.call-update) | async-done | bytes 1572880 | tf_op jit(solution)/shard_map/reduce_scatter | solution.py:71
  674.4 66.7 %reduce-scatter.11.cloned.1.call-done = bf16[1,384,2048]{2,1,0:T(8,128)(2,1)} async-done(((bf16[4,384,2048]{2,1,0:T(8,128)(2,1)}), bf16[1,384,2048]{2,1,0:T(8,128)(2,1)}) %reduce-scatter.11.cloned.1.call-update) | async-done | bytes 1572880 | tf_op jit(solution)/shard_map/reduce_scatter | solution.py:77
  741.1 0.0 copy-done.1
  (6 shorter events, 0.1 us)
Async XLA Ops:
  7.2 20.6 %copy-start = (bf16[128,2048]{1,0:T(8,128)(2,1)S(1)}, bf16[128,2048]{1,0:T(8,128)(2,1)}, u32[]{:S(2)}) copy-start(bf16[128,2048]{1,0:T(8,128)(2,1)} %param.7) | copy-start | bytes 1572868
  39.0 8.3 %copy-start.3 = (f32[128,8]{0,1:T(8,128)S(1)}, f32[128,8]{0,1:T(8,128)}, u32[]{:S(2)}) copy-start(f32[128,8]{0,1:T(8,128)} %param.10) | copy-start | bytes 12292
  39.0 8.5 %copy-start.2 = (bf16[128,2048]{1,0:T(8,128)(2,1)S(1)}, bf16[128,2048]{1,0:T(8,128)(2,1)}, u32[]{:S(2)}) copy-start(bf16[128,2048]{1,0:T(8,128)(2,1)} %param.8) | copy-start | bytes 1572868
  39.0 111.2 %all-to-all-start.1 = ((bf16[16,128,2048]{2,1,0:T(8,128)(2,1)}), bf16[16,128,2048]{2,1,0:T(8,128)(2,1)}, u32[]{:S(2)}, u32[]{:S(2)}) async-start(bf16[16,128,2048]{2,1,0:T(8,128)(2,1)} %bitcast.147), calls=%async_computation.1 | async-start | bytes 16777216 | tf_op jit(solution)/shard_map/all_to_all | solution.py:31
  150.2 63.9 %slice-start = ((s8[6291456]{0:T(1024)(128)(4,1)}), s8[2097152]{0:T(1024)(128)(4,1)S(1)}, s32[]{:S(2)}) async-start(s8[6291456]{0:T(1024)(128)(4,1)} %bitcast.150), calls=%async_computation.11 | async-start | bytes 4194304
  150.2 154.8 %all-to-all-start = ((bf16[16,128,2048]{2,1,0:T(8,128)(2,1)}), bf16[16,128,2048]{2,1,0:T(8,128)(2,1)}, u32[]{:S(2)}, u32[]{:S(2)}) async-start(bf16[16,128,2048]{2,1,0:T(8,128)(2,1)} %bitcast.146), calls=%async_computation | async-start | bytes 16777216 | tf_op jit(solution)/shard_map/all_to_all | solution.py:32
  202.6 11.5 %slice-start.1 = ((s8[6291456]{0:T(1024)(128)(4,1)}), s8[4194304]{0:T(1024)(128)(4,1)S(1)}, s32[]{:S(2)}) async-start(s8[6291456]{0:T(1024)(128)(4,1)} %bitcast.150), calls=%async_computation.12 | async-start | bytes 8388608
  352.2 125.1 %all-to-all-start.2 = ((bf16[16,128,2048]{2,1,0:T(8,128)(2,1)}), bf16[16,128,2048]{2,1,0:T(8,128)(2,1)}, u32[]{:S(2)}, u32[]{:S(2)}) async-start(bf16[16,128,2048]{2,1,0:T(8,128)(2,1)} %bitcast.148), calls=%async_computation.2 | async-start | bytes 16777216 | tf_op jit(solution)/shard_map/all_to_all | solution.py:88
  385.5 140.3 %reduce-scatter.5.cloned.1.call-start = ((), (), s32[]{:S(2)}) async-start(), calls=%async_computation.7 | async-start | bytes 6291456 | tf_op jit(solution)/shard_map/reduce_scatter | solution.py:91
  490.6 117.0 %reduce-scatter.7.cloned.1.call-start = ((), (), s32[]{:S(2)}) async-start(), calls=%async_computation.8 | async-start | bytes 7864320 | tf_op jit(solution)/shard_map/reduce_scatter | solution.py:65
  524.4 216.7 %copy-start.1 = (bf16[128,2048]{1,0:T(8,128)(2,1)S(1)}, bf16[128,2048]{1,0:T(8,128)(2,1)}, u32[]{:S(2)}) copy-start(bf16[128,2048]{1,0:T(8,128)(2,1)} %param.7) | copy-start | bytes 1572868
  524.4 150.0 %reduce-scatter.9.cloned.1.call-start = ((), (), s32[]{:S(2)}) async-start(), calls=%async_computation.9 | async-start | bytes 7864320 | tf_op jit(solution)/shard_map/reduce_scatter | solution.py:71
  525.2 215.9 %reduce-scatter.11.cloned.1.call-start = ((), (), s32[]{:S(2)}) async-start(), calls=%async_computation.10 | async-start | bytes 7864320 | tf_op jit(solution)/shard_map/reduce_scatter | solution.py:77
Sparse Core Ops, SparseCore 0:
  490.7 34.4 reduce-scatter.4
  528.3 79.2 reduce-scatter.6
  610.7 63.6 reduce-scatter.8
  677.4 63.6 reduce-scatter.10
where the time goes:
time: 757 us; the launch traced here: 748 us
  waiting for transfers between devices  478 us (63%)
  starting transfers between devices  94.1 us (12%)
  matrix products  92.8 us (12%)
  local copies, waits for them, and re-layouts  34.5 us (5%)
  other arithmetic  34.5 us (5%)
  between operations  14.1 us (2%)
    all_to_all x1, waiting for transfers between devices, body(): lax.all_to_all(going_home, 'expert', split_axis=0, concat_axis=0, tiled=T...  91.8 us
    all_to_all x1, waiting for transfers between devices, body(): lax.all_to_all(sent_rows, 'expert', split_axis=0, concat_axis=0, tiled=True)  90.9 us
    all_to_all x1, waiting for transfers between devices, body(): lax.all_to_all(sent_cots, 'expert', split_axis=0, concat_axis=0, tiled=True)  82.3 us
    reduce_scatter x1, waiting for transfers between devices, body(): lax.psum_scatter(rounded[0].astype(jnp.float32).astype(jnp.bfloat16), 're...  78.1 us
    reduce_scatter x1, waiting for transfers between devices, body(): lax.psum_scatter(rounded[1].astype(jnp.float32).astype(jnp.bfloat16), 're...  66.8 us
    reduce_scatter x1, waiting for transfers between devices, body(): lax.psum_scatter(rounded[2].astype(jnp.float32).astype(jnp.bfloat16), 're...  66.7 us
    all_to_all x1, starting transfers between devices, body(): lax.all_to_all(sent_cots, 'expert', split_axis=0, concat_axis=0, tiled=True)  52.4 us
    all_to_all x1, starting transfers between devices, body(): lax.all_to_all(going_home, 'expert', split_axis=0, concat_axis=0, tiled=T...  33.2 us
  transfers between devices with their start and end apart: 7, of which 6 were waited for; matrix products, arithmetic and copies ran while one was open for 9% of the time, Pallas kernels for 0%

commit v1 on v0

v1 whole, which is shorter than its diff:
```python
import functools

import jax
import jax.numpy as jnp
from jax import lax
from jax.experimental import pallas as pl
from jax.experimental.pallas import tpu as pltpu
from jax.sharding import PartitionSpec as P

MESH = pl.DeviceIdType.MESH
CAP = 32
BF = jnp.bfloat16


def gray(i):
    return i + i // 2 - 2 * (i // 3)


def dispatch_kernel(src_ref, meta_ref, out_ref, ag, mag, stage, rows,
                    ag_s, ag_r, mg_s, mg_r, x_s, x_r, f_s, f_r, o_s):
    e = lax.axis_index("expert")
    x = lax.axis_index("replica")
    c = lax.axis_index("tensor")
    y, z = e // 4, e % 4
    first = c == 0
    width = src_ref.shape[1]

    def chip(dy, dz):
        return ((y + dy) % 4) * 4 + (z + dz) % 4

    def axis_a(d):
        return jnp.where(first, 0, d), jnp.where(first, d, 0)

    def axis_b(d):
        return jnp.where(first, d, 0), jnp.where(first, 0, d)

    barrier = pltpu.get_barrier_semaphore()
    for d in (1, 2, 3):
        for dev in ((chip(0, d), x, c), (chip(d, 0), x, c), (e, (x + d) % 4, c)):
            pl.semaphore_signal(barrier, inc=1, device_id=dev, device_id_type=MESH)
    pl.semaphore_signal(barrier, inc=1, device_id=(e, x, 1 - c), device_id_type=MESH)
    pl.semaphore_wait(barrier, 10)

    def block_copies(src, msrc, by, bz, ty, tz, slot):
        home = chip(by, bz)
        landed = ((by - ty + 4) % 4) * 4 + (bz - tz + 4) % 4
        dev = (chip(ty, tz), x, c)
        return (
            pltpu.make_async_remote_copy(src_ref=msrc, dst_ref=mag.at[home], send_sem=mg_s.at[slot],
                                         recv_sem=mg_r.at[landed], device_id=dev, device_id_type=MESH),
            pltpu.make_async_remote_copy(src_ref=src, dst_ref=ag.at[home], send_sem=ag_s.at[slot],
                                         recv_sem=ag_r.at[landed], device_id=dev, device_id_type=MESH),
        )

    def wait_block(by, bz):
        rel = by * 4 + bz
        for cp in (
            pltpu.make_async_remote_copy(src_ref=meta_ref, dst_ref=mag.at[chip(by, bz)], send_sem=mg_s.at[0],
                                         recv_sem=mg_r.at[rel], device_id=(e, x, 1 - c), device_id_type=MESH),
            pltpu.make_async_remote_copy(src_ref=src_ref, dst_ref=ag.at[chip(by, bz)], send_sem=ag_s.at[0],
                                         recv_sem=ag_r.at[rel], device_id=(e, x, 1 - c), device_id_type=MESH),
        ):
            cp.wait_recv()

    for i, d in enumerate((1, 3, 2)):
        for ax, base in ((axis_a, 0), (axis_b, 3)):
            ty, tz = ax(d)
            for cp in block_copies(src_ref, meta_ref, 0, 0, ty, tz, base + i):
                cp.start()
    ag[e] = src_ref[...]
    mag[e] = meta_ref[...]

    def x_copy(r, home, d):
        return pltpu.make_async_remote_copy(
            src_ref=stage.at[r, (x + d) % 4], dst_ref=rows.at[c, home, x], send_sem=x_s.at[r * 3 + d - 1],
            recv_sem=x_r.at[r * 3 + d - 1], device_id=(e, (x + d) % 4, c), device_id_type=MESH)

    def x_landed(r, home, d):
        return pltpu.make_async_remote_copy(
            src_ref=stage.at[r, 0], dst_ref=rows.at[c, home, (x - d + 4) % 4], send_sem=x_s.at[r * 3 + d - 1],
            recv_sem=x_r.at[r * 3 + d - 1], device_id=(e, (x + d) % 4, c), device_id_type=MESH)

    def forward(r, home, kind):
        return pltpu.make_async_remote_copy(
            src_ref=rows.at[kind, home], dst_ref=rows.at[kind, home], send_sem=f_s.at[r], recv_sem=f_r.at[r],
            device_id=(e, x, 1 - c), device_id_type=MESH)

    def put(r, home, kind):
        return pltpu.make_async_copy(rows.at[kind, home], out_ref.at[kind, home], o_s.at[kind, r])

    slot_ids = lax.broadcasted_iota(jnp.int32, (CAP, 128), 0).astype(jnp.float32)

    def pick(r, home):
        m = mag[home, e].astype(jnp.float32)
        gsum = m[4:8] + m[8:12] + m[12:16]
        sel, scale = [], []
        for j in range(4):
            s = jnp.where(slot_ids == m[j:j + 1], 1.0, 0.0)
            sel.append(s)
            scale.append(jnp.sum(s * gsum[j:j + 1], axis=1, keepdims=True))
        sel = jnp.concatenate(sel, axis=0).astype(BF)
        scale = jnp.concatenate(scale, axis=0)
        scale = jnp.where(first, jnp.ones_like(scale), scale)
        for t in range(0, width, 512):
            got = jnp.dot(sel, ag[home, :, t:t + 512], preferred_element_type=jnp.float32) * scale
            stage[r, :, :, t:t + 512] = got.astype(BF).reshape(4, CAP, 512)

    lag = 2

    def finish(r):
        home = chip(gray(r // 4), gray(r % 4))
        for d in (1, 2, 3):
            x_landed(r, home, d).wait_recv()
        forward(r, home, c).start()
        put(r, home, c).start()

    def step(r, carry):
        dy, dz = gray(r // 4), gray(r % 4)
        home = chip(dy, dz)

        @pl.when((r >= 1) & (r <= 3))
        def _():
            ay, az = axis_a(gray(r % 4))
            wait_block(ay, az)
            for i, d in enumerate((1, 3, 2)):
                ty, tz = axis_b(d)
                for cp in block_copies(ag.at[chip(ay, az)], mag.at[chip(ay, az)], ay, az, ty, tz, 3 + r * 3 + i):
                    cp.start()

        @pl.when(jnp.where(first, dy, dz) != 0)
        def _():
            wait_block(dy, dz)

        pick(r, home)
        for d in (1, 3, 2):
            x_copy(r, home, d).start()
        rows[c, home, x] = stage[r, x]

        @pl.when(r >= lag)
        def _():
            finish(r - lag)
        return carry

    lax.fori_loop(0, 16, step, 0)
    for r in range(16 - lag, 16):
        finish(r)

    def drain(r, carry):
        home = chip(gray(r // 4), gray(r % 4))
        forward(r, home, 1 - c).wait_recv()
        put(r, home, 1 - c).start()
        return carry

    lax.fori_loop(0, 16, drain, 0)

    def close(r, carry):
        home = chip(gray(r // 4), gray(r % 4))
        forward(r, home, c).wait_send()
        put(r, home, 0).wait()
        put(r, home, 1).wait()
        for d in (1, 2, 3):
            x_copy(r, home, d).wait_send()
        return carry

    lax.fori_loop(0, 16, close, 0)
    for slot in range(15):
        for cp in block_copies(src_ref, meta_ref, 0, 0, 0, 1, slot):
            cp.wait_send()


def dispatch(src, meta):
    width = src.shape[1]
    return pl.pallas_call(
        dispatch_kernel,
        out_shape=jax.ShapeDtypeStruct((2, 16, 4, CAP, width), BF),
        in_specs=[pl.BlockSpec(memory_space=pltpu.VMEM)] * 2,
        out_specs=pl.BlockSpec(memory_space=pl.ANY),
        scratch_shapes=[
            pltpu.VMEM((16, 128, width), BF),
            pltpu.VMEM((16, 16, 16, 128), BF),
            pltpu.VMEM((16, 4, CAP, width), BF),
            pltpu.VMEM((2, 16, 4, CAP, width), BF),
            pltpu.SemaphoreType.DMA((15,)),
            pltpu.SemaphoreType.DMA((16,)),
            pltpu.SemaphoreType.DMA((15,)),
            pltpu.SemaphoreType.DMA((16,)),
            pltpu.SemaphoreType.DMA((48,)),
            pltpu.SemaphoreType.DMA((48,)),
            pltpu.SemaphoreType.DMA((16,)),
            pltpu.SemaphoreType.DMA((16,)),
            pltpu.SemaphoreType.DMA((2, 16)),
        ],
        compiler_params=pltpu.CompilerParams(collective_id=0, has_side_effects=True, vmem_limit_bytes=48 * 2**20),
    )(src, meta)


def routing(routes, gates):
    ids = jnp.arange(64, dtype=jnp.int32)
    hit = ids[:, None, None] == routes.T[None]
    mask = jnp.sum(hit.astype(jnp.float32), axis=1)
    gmap = jnp.sum(jnp.where(hit, gates.T[None], 0.0), axis=1)
    before = jnp.triu(jnp.ones((128, 128), BF), 1)
    rank = jnp.dot(mask.astype(BF), before, preferred_element_type=jnp.float32)
    rank = jnp.where(mask > 0, rank, 64.0)
    high = lax.reduce_precision(gmap, 8, 7)
    rest = gmap - high
    mid = lax.reduce_precision(rest, 8, 7)
    low = rest - mid
    return rank, jnp.stack([rank, high, mid, low]).astype(BF)


def body(tokens, cotangent, routes, gates, gate_weight, up_weight, down_weight):
    width = tokens.shape[1]
    x = lax.axis_index("replica")
    c = lax.axis_index("tensor")
    rank, maps = routing(routes, gates)
    meta = maps.reshape(4, 16, 4, 128).transpose(1, 0, 2, 3).reshape(16, 16, 128)
    rows = dispatch(jnp.where(c == 0, tokens, cotangent), meta)
    rows_in = rows[0].reshape(2048, width)
    cots_in = rows[1].reshape(2048, width)
    w_gate, w_up, w_down = gate_weight[x], up_weight[x], down_weight[x]
    f32 = dict(preferred_element_type=jnp.float32)
    gate_pre = jnp.dot(rows_in, w_gate, **f32)
    up_proj = jnp.dot(rows_in, w_up, **f32)
    hidden_grad = jnp.dot(cots_in, w_down.T, **f32)
    sig = jax.nn.sigmoid(gate_pre)
    act = gate_pre * sig
    hidden = (act * up_proj).astype(BF)
    gate_grad = (hidden_grad * up_proj * sig * (1.0 + gate_pre * (1.0 - sig))).astype(BF)
    up_grad = (hidden_grad * act).astype(BF)
    row_grads = (jnp.dot(gate_grad, w_gate.T, **f32) + jnp.dot(up_grad, w_up.T, **f32)).astype(BF)
    g_gate = jnp.dot(rows_in.T, gate_grad, **f32).astype(BF)
    g_up = jnp.dot(rows_in.T, up_grad, **f32).astype(BF)
    g_down = jnp.dot(hidden.T, cots_in, **f32).astype(BF)

    halves = lax.psum_scatter(row_grads, "tensor", scatter_dimension=1, tiled=True)
    back = lax.all_to_all(halves.reshape(16, 128, width // 2), "expert", split_axis=0, concat_axis=0, tiled=True)
    back = back.reshape(16, 4, CAP, width // 2)
    all_rank = lax.all_gather(rank.astype(BF), "replica", axis=0)
    own = lax.dynamic_index_in_dim(all_rank.reshape(4, 16, 4, 128), x, 2, keepdims=False)
    place = (own[:, :, None, :] == jnp.arange(CAP, dtype=jnp.float32)[None, None, :, None]).astype(BF)
    sums = jnp.einsum("bgst,gbsd->btd", place, back, preferred_element_type=jnp.float32).astype(BF)
    token_grad = lax.psum_scatter(sums, "replica", scatter_dimension=0, tiled=True)
    return token_grad.reshape(128, width // 2), g_gate[None], g_up[None], g_down[None]


def solution(mesh):
    in_specs = (
        P(("expert", "replica"), None),
        P(("expert", "replica"), None),
        P(("expert", "replica"), None),
        P(("expert", "replica"), None),
        P("expert", None, "tensor"),
        P("expert", None, "tensor"),
        P("expert", "tensor", None),
    )
    out_specs = (
        P(("expert", "replica"), "tensor"),
        P(("expert", "replica"), None, "tensor"),
        P(("expert", "replica"), None, "tensor"),
        P(("expert", "replica"), "tensor", None),
    )
    return jax.shard_map(body, mesh=mesh, in_specs=in_specs, out_specs=out_specs, check_vma=False)
```

time: 757 us -> 307 us (0.41)
  waiting for transfers between devices: 478 us -> 68.1 us
  Pallas kernels: 0 us -> 116 us
  starting transfers between devices: 94.1 us -> 6.97 us
  other arithmetic: 34.5 us -> 2.03 us
  local copies, waits for them, and re-layouts: 34.5 us -> 11.9 us
  matrix products: 92.8 us -> 74.3 us
  blocking collectives: 0 us -> 10 us
    all_to_all x3 -> x1, waiting for transfers between devices: 265 us -> 34.3 us  [body(): lax.all_to_all(halves.reshape(16, 128, width // 2), 'expert', split_axis=...]
    reduce_scatter x4 -> x2, waiting for transfers between devices: 212 us -> 33.8 us  [the longest x1 18.7 us: body(): lax.psum_scatter(row_grads, 'tensor', scatter_dimension=1, tiled=True)]
    pallas_call x0 -> x1, Pallas kernels: none -> 116 us  [dispatch(): pl.pallas_call(dispatch_kernel, out_shape=jax.ShapeDtypeStruct((2, 16, 4,...]
    all_to_all x3 -> x1, starting transfers between devices: 93.9 us -> 6.89 us  [body(): lax.all_to_all(halves.reshape(16, 128, width // 2), 'expert', split_axis=...]
    dot_general x8 -> x10, matrix products: 92.8 us -> 74.3 us  [the longest x1 10.5 us: body(): jnp.dot(up_grad, w_up.T, **f32)]
    another operation x3 -> x1, other arithmetic: 18.2 us -> 0.01 us
    gather x1 -> x0, local copies, waits for them, and re-layouts: 13.3 us -> none  [body(): gathered = returned[position].reshape(tok_rows, top_count, full_width)]
    scatter x1 -> x0, other arithmetic: 11.6 us -> none  [body(): sent_cots = blank_rows.at[position].set(scaled.reshape(-1, send_width))]
  transfers between devices with their start and end apart: 7 -> 3, of which waited for: 6 -> 3; matrix products, arithmetic and copies ran while one was open for 9% -> 9% of each run, Pallas kernels for 0% -> 0%
where the time goes in v1:
time: 307 us; the launch traced here: 303 us
  Pallas kernels  116 us (38%)
  matrix products  74.3 us (24%)
  waiting for transfers between devices  68.1 us (22%)
  between operations  14.2 us (5%)
  local copies, waits for them, and re-layouts  11.9 us (4%)
  blocking collectives  10 us (3%)
  starting transfers between devices  6.97 us (2%)
    pallas_call x1, Pallas kernels, dispatch(): pl.pallas_call(dispatch_kernel, out_shape=jax.ShapeDtypeStruct((2, 16, 4,...  116 us
    all_to_all x1, waiting for transfers between devices, body(): lax.all_to_all(halves.reshape(16, 128, width // 2), 'expert', split_axis=...  34.3 us
    reduce_scatter x1, waiting for transfers between devices, body(): lax.psum_scatter(row_grads, 'tensor', scatter_dimension=1, tiled=True)  18.7 us
    reduce_scatter x1, waiting for transfers between devices, body(): lax.psum_scatter(sums, 'replica', scatter_dimension=0, tiled=True)  15.1 us
    slice x1, local copies, waits for them, and re-layouts, body(): cots_in = rows[1].reshape(2048, width)  11.8 us
    dot_general x1, matrix products, body(): jnp.dot(up_grad, w_up.T, **f32)  10.5 us
    all_gather x1, blocking collectives, body(): all_rank = lax.all_gather(rank.astype(BF), 'replica', axis=0)  10 us
    dot_general x1, matrix products, body(): jnp.dot(gate_grad, w_gate.T, **f32) + jnp.dot(up_grad, w_up.T, **f32)  9.72 us
  transfers between devices with their start and end apart: 3, of which 3 were waited for; matrix products, arithmetic and copies ran while one was open for 9% of the time, Pallas kernels for 0%

profile of v1, /device:TPU:11, one launch (start us, length us, event | category | flops | bytes accessed | tf_op | source)
XLA Modules:
  0.0 303.0 jit_solution(1280591587148095524)
XLA Ops:
  7.2 0.0 reduce-scatter.3.cloned.1.call-start
  7.2 0.9 convert_reduce_fusion
  8.1 0.1 fusion.22
  8.3 1.1 broadcast_select_fusion.src_ref
  9.4 115.5 %shard_map.102 = bf16[2,16,4,32,2048]{4,3,2,1,0:T(8,128)(2,1)} custom-call(bf16[128,2048]{1,0:T(8,128)(2,1)S(1)} %broadcast_select_fusion.src_ref, bf16[16,16,128]{2,1,0:T(8,128)(2,1)S(1)} %bitcast.48), custom_call_target="tpu_custom_call" | custom-call | tf_op jit(solution)/shard_map/pallas_call | solution.py:173
  125.0 11.8 %fusion.39 = (bf16[1,16,4,32,2048]{4,3,2,1,0:T(8,128)(2,1)}, bf16[1,16,4,32,2048]{4,3,2,1,0:T(8,128)(2,1)}) fusion(bf16[2,16,4,32,2048]{4,3,2,1,0:T(8,128)(2,1)} %shard_map.102), kind=kLoop, calls=%fused_computation.57 | loop fusion | bytes 33554432 | tf_op jit(solution)/shard_map/slice | solution.py:220
  136.8 0.0 copy-start
  136.8 0.0 slice-start
  136.8 7.6 %fusion.13 = f32[2048,384]{1,0:T(8,128)S(1)} fusion(bf16[2048,2048]{1,0:T(8,128)(2,1)} %bitcast.53, bf16[4,2048,384]{2,1,0:T(8,128)(2,1)} %param.12, s32[]{:T(128)S(6)} %select_n.29), kind=kOutput, calls=%fused_computation.20 | convolution fusion | flops 3221225472 | bytes 13107204 | tf_op jit(solution)/shard_map/dot_general | solution.py:224
  144.4 0.0 copy-done
  144.5 0.0 copy-start.1
  144.5 0.0 slice-start.1
  144.5 7.2 %fusion.10 = f32[2048,384]{1,0:T(8,128)S(1)} fusion(bf16[2048,2048]{1,0:T(8,128)(2,1)S(1)} %bitcast.56, bf16[4,2048,384]{2,1,0:T(8,128)(2,1)} %param.11, s32[]{:T(128)S(6)} %select_n.29), kind=kOutput, calls=%fused_computation.17 | convolution fusion | flops 3221225472 | bytes 13107204 | tf_op jit(solution)/shard_map/dot_general | solution.py:223
  151.7 0.0 copy-start.3
  151.7 0.0 copy-done.1
  151.7 0.0 slice-done
  151.7 0.0 slice-done.1
  151.7 8.4 %multiply_convert_fusion.1 = (bf16[2048,384]{1,0:T(8,128)(2,1)S(1)}, bf16[2048,384]{1,0:T(8,128)(2,1)S(1)}) fusion(f32[2048,384]{1,0:T(8,128)S(1)} %fusion.10, f32[2048,384]{1,0:T(8,128)S(1)} %fusion.13, bf16[2048,2048]{1,0:T(8,128)(2,1)S(1)} %bitcast.52, bf16[4,384,2048]{2,1,0:T(8,128)(2,1)} %param.13, s32[]{:T(128)S(6)} %select_n.29), kind=kOutput, calls=%fused_computation.4 | convolution fusion | flops 3231449088 | bytes 19398660 | tf_op jit(solution)/shard_map/dot_general | solution.py:225
  160.1 0.0 copy-done.3
  160.1 9.7 %fusion.8 = f32[2048,2048]{1,0:T(8,128)} fusion(bf16[2048,384]{1,0:T(8,128)(2,1)S(1)} %get-tuple-element.9, bf16[4,2048,384]{2,1,0:T(8,128)(2,1)} %param.11, s32[]{:T(128)S(6)} %select_n.29), kind=kOutput, calls=%fused_computation.15 | convolution fusion | flops 3221225472 | bytes 19922948 | tf_op jit(solution)/shard_map/dot_general | solution.py:231
  169.9 10.5 %add_convert_fusion = bf16[2048,2048]{1,0:T(8,128)(2,1)} fusion(f32[2048,2048]{1,0:T(8,128)} %fusion.8, bf16[2048,384]{1,0:T(8,128)(2,1)S(1)} %get-tuple-element.8, bf16[4,2048,384]{2,1,0:T(8,128)(2,1)} %param.12, s32[]{:T(128)S(6)} %select_n.29), kind=kOutput, calls=%fused_computation | convolution fusion | flops 3229614080 | bytes 28311556 | tf_op jit(solution)/shard_map/dot_general | solution.py:231
  180.4 0.0 reduce-scatter.3.cloned.1.call-update
  180.4 18.7 %reduce-scatter.3.cloned.1.call-done = bf16[2048,1024]{1,0:T(8,128)(2,1)} async-done(((bf16[2048,2048]{1,0:T(8,128)(2,1)}), bf16[2048,1024]{1,0:T(8,128)(2,1)}) %reduce-scatter.3.cloned.1.call-update) | async-done | bytes 4194320 | tf_op jit(solution)/shard_map/reduce_scatter | solution.py:236
  199.1 6.9 %all-to-all-start = ((bf16[16,128,1024]{2,1,0:T(8,128)(2,1)}), bf16[16,128,1024]{2,1,0:T(8,128)(2,1)}, u32[]{:S(2)}, u32[]{:S(2)}) async-start(bf16[16,128,1024]{2,1,0:T(8,128)(2,1)} %bitcast.57), calls=%async_computation.1 | async-start | bytes 8388608 | tf_op jit(solution)/shard_map/all_to_all | solution.py:237
  206.0 0.0 reduce-scatter.5.cloned.1.call-start
  206.0 10.0 %all-gather = bf16[256,128]{1,0:T(8,128)(2,1)S(1)} all-gather(bf16[64,128]{1,0:T(8,128)(2,1)S(1)} %fusion.22), channel_id=2, replica_groups=mesh['expert'=16,'replica'=4,'tensor'=2] {'replica'}, dimensions={0}, use_global_device_ids=true | all-gather | bytes 81920 | tf_op jit(solution)/shard_map/all_gather | solution.py:239
  216.1 9.1 %fusion.4 = bf16[1,2048,384]{2,1,0:T(8,128)(2,1)} fusion(bf16[2048,2048]{1,0:T(8,128)(2,1)} %bitcast.54, bf16[2048,384]{1,0:T(8,128)(2,1)S(1)} %get-tuple-element.8), kind=kOutput, calls=%fused_computation.12 | convolution fusion | flops 3222011904 | bytes 11534336 | tf_op jit(solution)/shard_map/dot_general | solution.py:233
  225.2 34.3 %all-to-all-done = bf16[16,128,1024]{2,1,0:T(8,128)(2,1)} async-done(((bf16[16,128,1024]{2,1,0:T(8,128)(2,1)}), bf16[16,128,1024]{2,1,0:T(8,128)(2,1)}, u32[]{:S(2)}, u32[]{:S(2)}) %all-to-all-start) | async-done | bytes 4194336 | tf_op jit(solution)/shard_map/all_to_all | solution.py:237
  259.5 4.0 %bitcast_convert_fusion = bf16[4,128,1024]{2,1,0:T(8,128)(2,1)} fusion(bf16[16,4,32,1024]{3,2,1,0:T(8,128)(2,1)} %bitcast.14, f32[4,16,128]{2,1,0:T(8,128)S(1)} %bitcast.61), kind=kOutput, calls=%fused_computation.14 | convolution fusion | flops 537657344 | bytes 5275648 | tf_op jit(solution)/shard_map/bgst,gbsd->btd/dot_general | solution.py:242
  263.4 0.0 reduce-scatter.5.cloned.1.call-update
  263.5 0.0 copy-start.2
  263.5 0.0 copy-start.4
  263.5 9.2 %fusion.3 = bf16[1,2048,384]{2,1,0:T(8,128)(2,1)} fusion(bf16[2048,2048]{1,0:T(8,128)(2,1)} %bitcast.55, bf16[2048,384]{1,0:T(8,128)(2,1)S(1)} %get-tuple-element.9), kind=kOutput, calls=%fused_computation.11 | convolution fusion | flops 3222011904 | bytes 11534336 | tf_op jit(solution)/shard_map/dot_general | solution.py:232
  272.7 0.0 copy-done.2
  272.7 0.0 copy-done.4
  272.7 8.3 %fusion.5 = bf16[1,384,2048]{2,1,0:T(8,128)(2,1)} fusion(bf16[2048,2048]{1,0:T(8,128)(2,1)} %bitcast.49, f32[2048,384]{1,0:T(8,128)S(1)} %copy-done.2, f32[2048,384]{1,0:T(8,128)S(1)} %copy-done.4), kind=kOutput, calls=%fused_computation.13 | convolution fusion | flops 3226730496 | bytes 16252928 | tf_op jit(solution)/shard_map/dot_general | solution.py:234
  281.1 15.1 %reduce-scatter.5.cloned.1.call-done = bf16[1,128,1024]{2,1,0:T(8,128)(2,1)} async-done(((bf16[4,128,1024]{2,1,0:T(8,128)(2,1)}), bf16[1,128,1024]{2,1,0:T(8,128)(2,1)}) %reduce-scatter.5.cloned.1.call-update) | async-done | bytes 262160 | tf_op jit(solution)/shard_map/reduce_scatter | solution.py:243
  (6 shorter events, 0.1 us)
Async XLA Ops:
  7.2 191.9 %reduce-scatter.3.cloned.1.call-start = ((), (), s32[]{:S(2)}) async-start(), calls=%async_computation.3 | async-start | bytes 12582912 | tf_op jit(solution)/shard_map/reduce_scatter | solution.py:236
  136.8 7.7 %copy-start = (bf16[1,16,4,32,2048]{4,3,2,1,0:T(8,128)(2,1)S(1)}, bf16[1,16,4,32,2048]{4,3,2,1,0:T(8,128)(2,1)}, u32[]{:S(2)}) copy-start(bf16[1,16,4,32,2048]{4,3,2,1,0:T(8,128)(2,1)} %get-tuple-element.7) | copy-start | bytes 25165828
  136.8 14.9 %slice-start = ((s8[8388608]{0:T(1024)(128)(4,1)}), s8[4194304]{0:T(1024)(128)(4,1)S(1)}, s32[]{:S(2)}) async-start(s8[8388608]{0:T(1024)(128)(4,1)} %bitcast.50), calls=%async_computation.5 | async-start | bytes 8388608
  144.5 7.2 %copy-start.1 = (f32[2048,384]{1,0:T(8,128)}, f32[2048,384]{1,0:T(8,128)S(1)}, u32[]{:S(2)}) copy-start(f32[2048,384]{1,0:T(8,128)S(1)} %fusion.13) | copy-start | bytes 9437188
  144.5 7.2 %slice-start.1 = ((s8[8388608]{0:T(1024)(128)(4,1)}), s8[4194304]{0:T(1024)(128)(4,1)S(1)}, s32[]{:S(2)}) async-start(s8[8388608]{0:T(1024)(128)(4,1)} %bitcast.50), calls=%async_computation.6 | async-start | bytes 8388608
  151.7 8.5 %copy-start.3 = (f32[2048,384]{1,0:T(8,128)}, f32[2048,384]{1,0:T(8,128)S(1)}, u32[]{:S(2)}) copy-start(f32[2048,384]{1,0:T(8,128)S(1)} %fusion.10) | copy-start | bytes 9437188
  199.1 60.3 %all-to-all-start = ((bf16[16,128,1024]{2,1,0:T(8,128)(2,1)}), bf16[16,128,1024]{2,1,0:T(8,128)(2,1)}, u32[]{:S(2)}, u32[]{:S(2)}) async-start(bf16[16,128,1024]{2,1,0:T(8,128)(2,1)} %bitcast.57), calls=%async_computation.1 | async-start | bytes 8388608 | tf_op jit(solution)/shard_map/all_to_all | solution.py:237
  206.0 90.2 %reduce-scatter.5.cloned.1.call-start = ((), (), s32[]{:S(2)}) async-start(), calls=%async_computation.4 | async-start | bytes 1310720 | tf_op jit(solution)/shard_map/reduce_scatter | solution.py:243
  263.5 9.3 %copy-start.2 = (f32[2048,384]{1,0:T(8,128)S(1)}, f32[2048,384]{1,0:T(8,128)}, u32[]{:S(2)}) copy-start(f32[2048,384]{1,0:T(8,128)} %copy-done.1) | copy-start | bytes 9437188
  263.5 9.3 %copy-start.4 = (f32[2048,384]{1,0:T(8,128)S(1)}, f32[2048,384]{1,0:T(8,128)}, u32[]{:S(2)}) copy-start(f32[2048,384]{1,0:T(8,128)} %copy-done.3) | copy-start | bytes 9437188
Sparse Core Ops, SparseCore 0:
  180.5 18.5 reduce-scatter.2
  263.6 32.5 reduce-scatter.4

commit v2 on v1

v2 whole, which is shorter than its diff:
```python
import jax
import jax.numpy as jnp
from jax import lax
from jax.experimental import pallas as pl
from jax.experimental.pallas import tpu as pltpu
from jax.sharding import PartitionSpec as P

MESH = pl.DeviceIdType.MESH
CAP = 32
BF = jnp.bfloat16
F32 = jnp.float32
LAG = 3
SLOTS = 8


def gray(i):
    return i + i // 2 - 2 * (i // 3)


def dot(a, b, ca, cb):
    return lax.dot_general(a, b, (((ca,), (cb,)), ((), ())), preferred_element_type=F32)


def layer_kernel(src_ref, meta_ref, rank_ref, wg_ref, wu_ref, wd_ref,
                 tok_ref, og_ref, ou_ref, od_ref,
                 ag, mag, stage, rows, wgu, wd, hid, grads, gu, hg, psend, precv, own, back,
                 xrank, place, xsend, xrecv, gtile, dtile,
                 ag_s, ag_r, mg_s, mg_r, x_s, x_r, f_s, f_r, p_s, p_r, b_s, b_r, k_s, k_r, t_s, t_r, w_s, og_s, od_s):
    e = lax.axis_index("expert")
    x = lax.axis_index("replica")
    c = lax.axis_index("tensor")
    y, z = e // 4, e % 4
    first = c == 0
    width = src_ref.shape[1]
    half = width // 2
    hidden = wd.shape[0]

    def chip(dy, dz):
        return ((y + dy) % 4) * 4 + (z + dz) % 4

    def remote(src, dst, send, recv, dev):
        return pltpu.make_async_remote_copy(src_ref=src, dst_ref=dst, send_sem=send, recv_sem=recv,
                                            device_id=dev, device_id_type=MESH)

    def axis_a(d):
        return jnp.where(first, 0, d), jnp.where(first, d, 0)

    def axis_b(d):
        return jnp.where(first, d, 0), jnp.where(first, 0, d)

    partner = (e, x, 1 - c)

    def weights():
        return (pltpu.make_async_copy(wg_ref.at[x], wgu.at[:, pl.ds(0, hidden)], w_s.at[0]),
                pltpu.make_async_copy(wu_ref.at[x], wgu.at[:, pl.ds(hidden, hidden)], w_s.at[1]),
                pltpu.make_async_copy(wd_ref.at[x], wd, w_s.at[2]))

    for cp in weights():
        cp.start()

    barrier = pltpu.get_barrier_semaphore()
    for rel in range(1, 16):
        pl.semaphore_signal(barrier, inc=1, device_id=(chip(rel // 4, rel % 4), x, c), device_id_type=MESH)
    for d in (1, 2, 3):
        pl.semaphore_signal(barrier, inc=1, device_id=(e, (x + d) % 4, c), device_id_type=MESH)
    pl.semaphore_signal(barrier, inc=1, device_id=partner, device_id_type=MESH)
    pl.semaphore_wait(barrier, 19)

    def block_copies(src, msrc, by, bz, ty, tz, slot):
        home = chip(by, bz)
        landed = ((by - ty + 4) % 4) * 4 + (bz - tz + 4) % 4
        dev = (chip(ty, tz), x, c)
        return (remote(msrc, mag.at[home], mg_s.at[slot], mg_r.at[landed], dev),
                remote(src, ag.at[home], ag_s.at[slot], ag_r.at[landed], dev))

    def wait_block(by, bz):
        rel, home = by * 4 + bz, chip(by, bz)
        remote(meta_ref, mag.at[home], mg_s.at[0], mg_r.at[rel], partner).wait_recv()
        remote(src_ref, ag.at[home], ag_s.at[0], ag_r.at[rel], partner).wait_recv()

    for i, d in enumerate((1, 3, 2)):
        for ax, base in ((axis_a, 0), (axis_b, 3)):
            ty, tz = ax(d)
            for cp in block_copies(src_ref, meta_ref, 0, 0, ty, tz, base + i):
                cp.start()

    def rank_copy(d):
        return remote(rank_ref.at[(x + d) % 4], xrank.at[x], k_s.at[d - 1], k_r.at[d - 1], (e, (x + d) % 4, c))

    def rank_landed(d):
        return remote(rank_ref.at[0], xrank.at[(x - d + 4) % 4], k_s.at[d - 1], k_r.at[d - 1], partner)

    for d in (1, 2, 3):
        rank_copy(d).start()
    xrank[x] = rank_ref[x]
    ag[e] = src_ref[...]
    mag[e] = meta_ref[...]

    def x_copy(r, home, d):
        return remote(stage.at[r % SLOTS, (x + d) % 4], rows.at[c, home, x], x_s.at[r * 3 + d - 1],
                      x_r.at[r * 3 + d - 1], (e, (x + d) % 4, c))

    def x_landed(r, home, d):
        return remote(stage.at[0, 0], rows.at[c, home, (x - d + 4) % 4], x_s.at[r * 3 + d - 1],
                      x_r.at[r * 3 + d - 1], partner)

    def forward(r, home, kind):
        return remote(rows.at[kind, home], rows.at[kind, home], f_s.at[r], f_r.at[r], partner)

    slot_ids = lax.broadcasted_iota(jnp.int32, (CAP, 128), 0).astype(F32)

    def pick(r, home):
        m = mag[home, e].astype(F32)
        gsum = m[4:8] + m[8:12] + m[12:16]
        sel, scale = [], []
        for j in range(4):
            s = jnp.where(slot_ids == m[j:j + 1], 1.0, 0.0)
            sel.append(s)
            scale.append(jnp.sum(s * gsum[j:j + 1], axis=1, keepdims=True))
        sel = jnp.concatenate(sel, axis=0).astype(BF)
        scale = jnp.concatenate(scale, axis=0)
        scale = jnp.where(first, jnp.ones_like(scale), scale)
        for t in range(0, width, 512):
            got = dot(sel, ag[home, :, t:t + 512], 1, 0) * scale
            stage[r % SLOTS, :, :, t:t + 512] = got.astype(BF).reshape(4, CAP, 512)

    def pair_copy(q):
        return remote(psend.at[q % 2], precv.at[q], p_s.at[q], p_r.at[q], partner)

    def back_copy(q, dz):
        landed = ((4 - q) % 4) * 4 + (4 - dz) % 4
        return remote(precv.at[q, (z + dz) % 4], back.at[e], b_s.at[q * 4 + dz], b_r.at[landed],
                      (chip(q, dz), x, c))

    def back_landed(dy, dz):
        return remote(precv.at[0, 0], back.at[chip(dy, dz)], b_s.at[0], b_r.at[dy * 4 + dz], partner)

    def chunk(q):
        ya = (y + q) % 4
        for i in range(4):
            r = q * 4 + i
            forward(r, chip(q, gray(i)), 1 - c).wait_recv()

        @pl.when(q == 0)
        def _():
            for cp in weights():
                cp.wait()

        gu[...] = dot(rows[0, pl.ds(ya * 4, 4)].reshape(512, width), wgu[...], 1, 0)
        hg[...] = dot(rows[1, pl.ds(ya * 4, 4)].reshape(512, width), wd[...], 1, 1)

        def act(i, carry):
            at = pl.multiple_of(i * 128, 128)
            to = pl.multiple_of(ya * 512 + i * 128, 128)
            for t in range(0, hidden, 128):
                g = gu[pl.ds(at, 128), t:t + 128]
                u = gu[pl.ds(at, 128), hidden + t:hidden + t + 128]
                h = hg[pl.ds(at, 128), t:t + 128]
                s = jax.nn.sigmoid(g)
                a = g * s
                hid[pl.ds(to, 128), t:t + 128] = (a * u).astype(BF)
                grads[pl.ds(to, 128), t:t + 128] = (h * u * s * (1.0 + g * (1.0 - s))).astype(BF)
                grads[pl.ds(to, 128), hidden + t:hidden + t + 128] = (h * a).astype(BF)
            return carry

        lax.fori_loop(0, 4, act, 0)

        @pl.when(q >= 2)
        def _():
            pair_copy(q - 2).wait_send()

        mine = grads[pl.ds(pl.multiple_of(ya * 512, 512), 512), :]
        for t in range(0, half, 512):
            w = wgu[pl.ds(pl.multiple_of((1 - c) * half + t, 512), 512), :]
            psend[q % 2, :, :, :, t:t + 512] = dot(mine, w, 1, 1).astype(BF).reshape(4, 4, CAP, 512)
        pair_copy(q).start()
        for t in range(0, half, 512):
            w = wgu[pl.ds(pl.multiple_of(c * half + t, 512), 512), :]
            own[:, t:t + 512] = dot(mine, w, 1, 1)
        pair_copy(q).wait_recv()
        for i in range(4):
            for t in range(0, half, 512):
                both = own[i * 128:(i + 1) * 128, t:t + 512].reshape(4, CAP, 512) + precv[q, i, :, :, t:t + 512].astype(F32)
                precv[q, i, :, :, t:t + 512] = both.astype(BF)
        for dz in range(4):
            @pl.when((q != 0) | (dz != 0))
            def _():
                back_copy(q, dz).start()

        @pl.when(q == 0)
        def _():
            back[e] = precv[0, z]

    def finish(r):
        home = chip(r // 4, gray(r % 4))
        for d in (1, 2, 3):
            x_landed(r, home, d).wait_recv()
        forward(r, home, c).start()

    def produce(r):
        dy, dz = r // 4, gray(r % 4)
        home = chip(dy, dz)

        @pl.when((r >= 1) & (r <= 3))
        def _():
            ay, az = axis_a(gray(r % 4))
            wait_block(ay, az)
            for i, d in enumerate((1, 3, 2)):
                ty, tz = axis_b(d)
                for cp in block_copies(ag.at[chip(ay, az)], mag.at[chip(ay, az)], ay, az, ty, tz, 3 + r * 3 + i):
                    cp.start()

        @pl.when(jnp.where(first, dy, dz) != 0)
        def _():
            wait_block(dy, dz)

        @pl.when(r >= SLOTS)
        def _():
            for d in (1, 2, 3):
                x_copy(r - SLOTS, home, d).wait_send()

        pick(r, home)
        for d in (1, 3, 2):
            x_copy(r, home, d).start()
        rows[c, home, x] = stage[r % SLOTS, x]

    def step(s, carry):
        @pl.when(s < 16)
        def _():
            produce(s)

        @pl.when((s >= LAG) & (s < 16 + LAG))
        def _():
            finish(s - LAG)

        @pl.when((s > LAG) & ((s - LAG) % 4 == 0))
        def _():
            chunk((s - LAG) // 4 - 1)
        return carry

    lax.fori_loop(0, 17 + LAG, step, 0)

    for d in (1, 2, 3):
        rank_landed(d).wait_recv()
    for k in range(4):
        m = xrank[k].astype(F32)
        for g in range(16):
            place[k, g * CAP:(g + 1) * CAP, :] = jnp.where(slot_ids == m[g:g + 1], 1.0, 0.0).astype(BF)

    def grad_out(t):
        at = pl.ds(pl.multiple_of(t * 512, 512), 512)
        return (pltpu.make_async_copy(gtile.at[t % 2, :, pl.ds(0, hidden)], og_ref.at[0, at, :], og_s.at[0, t]),
                pltpu.make_async_copy(gtile.at[t % 2, :, pl.ds(hidden, hidden)], ou_ref.at[0, at, :], og_s.at[1, t]),
                pltpu.make_async_copy(dtile.at[t % 2], od_ref.at[0, :, at], od_s.at[t]))

    for t in range(4):
        cols = slice(t * 512, (t + 1) * 512)
        if t >= 2:
            for cp in grad_out(t - 2):
                cp.wait()
        gtile[t % 2] = dot(rows[0, :, :, :, cols].reshape(2048, 512), grads[...], 0, 0).astype(BF)
        dtile[t % 2] = dot(hid[...], rows[1, :, :, :, cols].reshape(2048, 512), 0, 0).astype(BF)
        for cp in grad_out(t):
            cp.start()

    def waits(rel, carry):
        back_landed(rel // 4, rel % 4).wait_recv()
        return carry

    lax.fori_loop(1, 16, waits, 0)

    def combine(k, t):
        return dot(place[k], back[:, pl.ds(k, 1), :, t:t + 512].reshape(512, 512), 0, 0)

    def sum_copy(d):
        return remote(xsend.at[d - 1], xrecv.at[d - 1], t_s.at[d - 1], t_r.at[d - 1], (e, (x + d) % 4, c))

    for d in (2, 1, 3):
        for t in range(0, half, 512):
            xsend[d - 1, :, t:t + 512] = combine((x + d) % 4, t).astype(BF)
        sum_copy(d).start()
    for t in range(0, half, 512):
        own[0:128, t:t + 512] = combine(x, t)
    for d in (1, 3, 2):
        sum_copy(d).wait_recv()
    total = own[0:128, :]
    for d in (1, 2, 3):
        total = total + xrecv[d - 1].astype(F32)
    tok_ref[...] = total.astype(BF)

    def close(r, carry):
        home = chip(r // 4, gray(r % 4))
        forward(r, home, c).wait_send()

        @pl.when(r >= 16 - SLOTS)
        def _():
            for d in (1, 2, 3):
                x_copy(r, home, d).wait_send()

        @pl.when(r >= 1)
        def _():
            back_copy(r // 4, r % 4).wait_send()
        return carry

    lax.fori_loop(0, 16, close, 0)
    for slot in range(15):
        for cp in block_copies(src_ref, meta_ref, 0, 0, 0, 1, slot):
            cp.wait_send()
    for d in (1, 2, 3):
        rank_copy(d).wait_send()
        sum_copy(d).wait_send()
    for q in (2, 3):
        pair_copy(q).wait_send()
    for t in (2, 3):
        for cp in grad_out(t):
            cp.wait()


def layer(src, meta, ranks, w_gate, w_up, w_down):
    width = src.shape[1]
    hidden = w_gate.shape[2]
    half = width // 2
    dma = pltpu.SemaphoreType.DMA
    vmem = pl.BlockSpec(memory_space=pltpu.VMEM)
    hbm = pl.BlockSpec(memory_space=pl.ANY)
    return pl.pallas_call(
        layer_kernel,
        out_shape=(
            jax.ShapeDtypeStruct((128, half), BF),
            jax.ShapeDtypeStruct((1, width, hidden), BF),
            jax.ShapeDtypeStruct((1, width, hidden), BF),
            jax.ShapeDtypeStruct((1, hidden, width), BF),
        ),
        in_specs=[vmem, vmem, vmem, hbm, hbm, hbm],
        out_specs=(vmem, hbm, hbm, hbm),
        scratch_shapes=[
            pltpu.VMEM((16, 128, width), BF),
            pltpu.VMEM((16, 16, 16, 128), BF),
            pltpu.VMEM((SLOTS, 4, CAP, width), BF),
            pltpu.VMEM((2, 16, 4, CAP, width), BF),
            pltpu.VMEM((width, 2 * hidden), BF),
            pltpu.VMEM((hidden, width), BF),
            pltpu.VMEM((2048, hidden), BF),
            pltpu.VMEM((2048, 2 * hidden), BF),
            pltpu.VMEM((512, 2 * hidden), F32),
            pltpu.VMEM((512, hidden), F32),
            pltpu.VMEM((2, 4, 4, CAP, half), BF),
            pltpu.VMEM((4, 4, 4, CAP, half), BF),
            pltpu.VMEM((512, half), F32),
            pltpu.VMEM((16, 4, CAP, half), BF),
            pltpu.VMEM((4, 16, 128), BF),
            pltpu.VMEM((4, 512, 128), BF),
            pltpu.VMEM((3, 128, half), BF),
            pltpu.VMEM((3, 128, half), BF),
            pltpu.VMEM((2, 512, 2 * hidden), BF),
            pltpu.VMEM((2, hidden, 512), BF),
            dma((15,)), dma((16,)), dma((15,)), dma((16,)), dma((48,)), dma((48,)), dma((16,)), dma((16,)),
            dma((4,)), dma((4,)), dma((16,)), dma((16,)), dma((3,)), dma((3,)), dma((3,)), dma((3,)),
            dma((3,)), dma((2, 4)), dma((4,)),
        ],
        compiler_params=pltpu.CompilerParams(collective_id=0, has_side_effects=True, vmem_limit_bytes=67043328),
    )(src, meta, ranks, w_gate, w_up, w_down)


def routing(routes, gates):
    ids = jnp.arange(64, dtype=jnp.int32)
    hit = ids[:, None, None] == routes.T[None]
    mask = jnp.sum(hit.astype(F32), axis=1)
    gmap = jnp.sum(jnp.where(hit, gates.T[None], 0.0), axis=1)
    before = jnp.triu(jnp.ones((128, 128), BF), 1)
    rank = jnp.dot(mask.astype(BF), before, preferred_element_type=F32)
    rank = jnp.where(mask > 0, rank, 64.0)
    high = lax.reduce_precision(gmap, 8, 7)
    rest = gmap - high
    mid = lax.reduce_precision(rest, 8, 7)
    low = rest - mid
    return jnp.stack([rank, high, mid, low]).astype(BF)


def body(tokens, cotangent, routes, gates, gate_weight, up_weight, down_weight):
    c = lax.axis_index("tensor")
    maps = routing(routes, gates).reshape(4, 16, 4, 128)
    meta = maps.transpose(1, 0, 2, 3).reshape(16, 16, 128)
    ranks = maps[0].transpose(1, 0, 2)
    src = jnp.where(c == 0, tokens, cotangent)
    return layer(src, meta, ranks, gate_weight, up_weight, down_weight)


def solution(mesh):
    in_specs = (
        P(("expert", "replica"), None),
        P(("expert", "replica"), None),
        P(("expert", "replica"), None),
        P(("expert", "replica"), None),
        P("expert", None, "tensor"),
        P("expert", None, "tensor"),
        P("expert", "tensor", None),
    )
    out_specs = (
        P(("expert", "replica"), "tensor"),
        P(("expert", "replica"), None, "tensor"),
        P(("expert", "replica"), None, "tensor"),
        P(("expert", "replica"), "tensor", None),
    )
    return jax.shard_map(body, mesh=mesh, in_specs=in_specs, out_specs=out_specs, check_vma=False)
```

time: 307 us -> 203 us (0.66)
  matrix products: 74.3 us -> 0.13 us
  Pallas kernels: 116 us -> 189 us
  waiting for transfers between devices: 68.1 us -> 0 us
  between operations: 14.2 us -> 0.67 us
  blocking collectives: 10 us -> 0 us
  starting transfers between devices: 6.97 us -> 0 us
    dot_general x10 -> x1, matrix products: 74.3 us -> 0.13 us  [routing(): rank = jnp.dot(mask.astype(BF), before, preferred_element_type=F32)]
    pallas_call x1, Pallas kernels: 116 us -> 189 us  [layer(): pl.pallas_call(layer_kernel, out_shape=(jax.ShapeDtypeStruct((128, half),...]
    all_to_all x1 -> x0, waiting for transfers between devices: 34.3 us -> none  [body(): lax.all_to_all(halves.reshape(16, 128, width // 2), 'expert', split_axis=...]
    reduce_scatter x2 -> x0, waiting for transfers between devices: 33.8 us -> none  [the longest x1 18.7 us: body(): lax.psum_scatter(row_grads, 'tensor', scatter_dimension=1, tiled=True)]
    slice x1 -> x0, local copies, waits for them, and re-layouts: 11.8 us -> none  [body(): cots_in = rows[1].reshape(2048, width)]
    all_gather x1 -> x0, blocking collectives: 10 us -> none  [body(): all_rank = lax.all_gather(rank.astype(BF), 'replica', axis=0)]
    unnamed x14 -> x8, local copies, waits for them, and re-layouts: 0.03 us -> 7.62 us
    all_to_all x1 -> x0, starting transfers between devices: 6.89 us -> none  [body(): lax.all_to_all(halves.reshape(16, 128, width // 2), 'expert', split_axis=...]
  transfers between devices with their start and end apart: 3 -> 0, of which waited for: 3 -> 0; matrix products, arithmetic and copies ran while one was open for 9% -> 0% of each run, Pallas kernels for 0% -> 0%
where the time goes in v2:
time: 203 us; the launch traced here: 201 us
  Pallas kernels  189 us (93%)
  local copies, waits for them, and re-layouts  8.9 us (4%)
  other arithmetic  2.78 us (1%)
    pallas_call x1, Pallas kernels, layer(): pl.pallas_call(layer_kernel, out_shape=(jax.ShapeDtypeStruct((128, half),...  189 us
    unnamed x8, local copies, waits for them, and re-layouts  7.62 us

profile of v2, /device:TPU:11, one launch (start us, length us, event | category | flops | bytes accessed | tf_op | source)
XLA Modules:
  0.0 201.3 jit_solution(675331936282880917)
XLA Ops:
  0.6 0.9 convert_reduce_fusion
  1.5 0.1 fusion
  1.6 0.6 copy.32
  2.3 0.7 copy.23
  2.9 1.9 broadcast_select_fusion.src_ref
  4.8 188.9 %shard_map.102 = (bf16[128,1024]{1,0:T(8,128)(2,1)}, bf16[1,2048,384]{2,1,0:T(8,128)(2,1)}, bf16[1,2048,384]{2,1,0:T(8,128)(2,1)}, bf16[1,384,2048]{2,1,0:T(8,128)(2,1)}) custom-call(bf16[128,2048]{1,0:T(8,128)(2,1)} %broadcast_select_fusion.src_ref, bf16[16,16,128]{2,1,0:T(8,128)(2,1)} %bitcast.11, bf16[4,16,128]{2,1,0:T(8,128)(2,1)} %bitcast.15, ...), custom_call_target="tpu_custom_call" | custom-call | tf_op jit(solution)/shard_map/pallas_call | solution.py:326
  193.7 1.7 copy.37
  195.4 0.0 copy-start.1
  195.4 2.8 %copy.38 = bf16[1,2048,384]{2,1,0:T(8,128)(2,1)} copy(bf16[1,2048,384]{2,1,0:T(8,128)(2,1)} %get-tuple-element.14) | data formatting | bytes 3145728
  198.2 0.0 copy-done.1
  198.2 0.0 copy-start
  198.2 1.1 copy.39
  199.4 0.8 copy-done
  200.2 1.1 copy.40
  (3 shorter events, 0.0 us)
Async XLA Ops:
  195.4 2.8 %copy-start.1 = (bf16[1,2048,384]{2,1,0:T(8,128)(2,1)S(1)}, bf16[1,2048,384]{2,1,0:T(8,128)(2,1)}, u32[]{:S(2)}) copy-start(bf16[1,2048,384]{2,1,0:T(8,128)(2,1)} %get-tuple-element.15) | copy-start | bytes 4718596
  198.2 2.0 copy-start

commit v3 on v2

v3 whole, which is shorter than its diff:
```python
import jax
import jax.numpy as jnp
from jax import lax
from jax.experimental import pallas as pl
from jax.experimental.pallas import tpu as pltpu
from jax.sharding import PartitionSpec as P

MESH = pl.DeviceIdType.MESH
CAP = 32
BF = jnp.bfloat16
F32 = jnp.float32
LAG = 4
SLOTS = 8
ORDER = ((0, 0), (0, 1), (1, 0), (0, 2), (2, 0), (1, 1), (3, 3), (2, 1),
         (1, 2), (3, 2), (2, 3), (2, 2), (1, 3), (3, 1), (0, 3), (3, 0))
EARLY = 14


def entry(r, column):
    if isinstance(r, int):
        return ORDER[r][column]
    found = 0
    for k, pair in enumerate(ORDER):
        if pair[column]:
            found = found + jnp.where(r == k, pair[column], 0)
    return found


def offset(r):
    return entry(r, 0), entry(r, 1)


def dot(a, b, ca, cb):
    return lax.dot_general(a, b, (((ca,), (cb,)), ((), ())), preferred_element_type=F32)


def layer_kernel(token_ref, cot_ref, meta_ref, rank_ref, wg_ref, wu_ref, wd_ref,
                 tok_ref, og_ref, ou_ref, od_ref,
                 ag, mag, stage, rows, wgu, wd, hid, grads, gu, hg, psend, precv, own, back,
                 last, xrank, place, lplace, xsend, xrecv, gtile, dtile,
                 ag_s, ag_r, mg_s, mg_r, x_s, x_r, f_s, f_r, p_s, p_r, b_s, b_r, l_s, l_r, k_s, k_r, t_s, t_r, w_s, og_s, od_s, i_s):
    e = lax.axis_index("expert")
    x = lax.axis_index("replica")
    c = lax.axis_index("tensor")
    y, z = e // 4, e % 4
    first = c == 0
    width = token_ref.shape[1]
    half = width // 2
    hidden = wd.shape[0]

    def chip(dy, dz):
        return ((y + dy + 4) % 4) * 4 + (z + dz + 4) % 4

    def remote(src, dst, send, recv, dev):
        return pltpu.make_async_remote_copy(src_ref=src, dst_ref=dst, send_sem=send, recv_sem=recv,
                                            device_id=dev, device_id_type=MESH)

    def axis_a(d):
        return jnp.where(first, 0, d), jnp.where(first, d, 0)

    def axis_b(d):
        return jnp.where(first, d, 0), jnp.where(first, 0, d)

    partner = (e, x, 1 - c)

    def weights():
        return (pltpu.make_async_copy(wg_ref.at[x], wgu.at[:, pl.ds(0, hidden)], w_s.at[0]),
                pltpu.make_async_copy(wu_ref.at[x], wgu.at[:, pl.ds(hidden, hidden)], w_s.at[1]),
                pltpu.make_async_copy(wd_ref.at[x], wd, w_s.at[2]))

    @pl.when(first)
    def _():
        pltpu.make_async_copy(token_ref, ag.at[e], i_s).start()

    @pl.when(jnp.logical_not(first))
    def _():
        pltpu.make_async_copy(cot_ref, ag.at[e], i_s).start()

    barrier = pltpu.get_barrier_semaphore()
    for rel in range(1, 16):
        pl.semaphore_signal(barrier, inc=1, device_id=(chip(rel // 4, rel % 4), x, c), device_id_type=MESH)
    for d in (1, 2, 3):
        pl.semaphore_signal(barrier, inc=1, device_id=(e, (x + d) % 4, c), device_id_type=MESH)
        for r in (14, 15):
            dy, dz = ORDER[r]
            pl.semaphore_signal(barrier, inc=1, device_id=(chip(dy, dz), (x + d) % 4, c), device_id_type=MESH)
            pl.semaphore_signal(barrier, inc=1, device_id=(chip(-dy, -dz), (x + d) % 4, c), device_id_type=MESH)
    pl.semaphore_signal(barrier, inc=1, device_id=partner, device_id_type=MESH)
    pltpu.make_async_copy(token_ref, ag.at[e], i_s).wait()
    pl.semaphore_wait(barrier, 31)

    def block_copies(src, msrc, by, bz, ty, tz, slot):
        home = chip(by, bz)
        landed = ((by - ty + 4) % 4) * 4 + (bz - tz + 4) % 4
        dev = (chip(ty, tz), x, c)
        return (remote(msrc, mag.at[home], mg_s.at[slot], mg_r.at[landed], dev),
                remote(src, ag.at[home], ag_s.at[slot], ag_r.at[landed], dev))

    def wait_block(by, bz):
        rel, home = by * 4 + bz, chip(by, bz)
        remote(meta_ref, mag.at[home], mg_s.at[0], mg_r.at[rel], partner).wait_recv()
        remote(ag.at[e], ag.at[home], ag_s.at[0], ag_r.at[rel], partner).wait_recv()

    for i, d in enumerate((1, 3, 2)):
        for ax, base in ((axis_a, 0), (axis_b, 3)):
            ty, tz = ax(d)
            for cp in block_copies(ag.at[e], meta_ref, 0, 0, ty, tz, base + i):
                cp.start()

    def rank_copy(d):
        return remote(rank_ref.at[(x + d) % 4], xrank.at[x], k_s.at[d - 1], k_r.at[d - 1], (e, (x + d) % 4, c))

    def rank_landed(d):
        return remote(rank_ref.at[0], xrank.at[(x - d + 4) % 4], k_s.at[d - 1], k_r.at[d - 1], partner)

    for d in (1, 2, 3):
        rank_copy(d).start()
    xrank[x] = rank_ref[x]
    mag[e] = meta_ref[...]
    for cp in weights():
        cp.start()

    def x_copy(r, d):
        return remote(stage.at[r % SLOTS, (x + d) % 4], rows.at[c, r, x], x_s.at[r * 3 + d - 1],
                      x_r.at[r * 3 + d - 1], (e, (x + d) % 4, c))

    def x_landed(r, d):
        return remote(stage.at[0, 0], rows.at[c, r, (x - d + 4) % 4], x_s.at[r * 3 + d - 1],
                      x_r.at[r * 3 + d - 1], partner)

    def forward(r, kind):
        return remote(rows.at[kind, r], rows.at[kind, r], f_s.at[r], f_r.at[r], partner)

    slot_ids = lax.broadcasted_iota(jnp.int32, (CAP, 128), 0).astype(F32)

    def pick(r, home):
        m = mag[home, e].astype(F32)
        gsum = m[4:8] + m[8:12] + m[12:16]
        sel, scale = [], []
        for j in range(4):
            s = jnp.where(slot_ids == m[j:j + 1], 1.0, 0.0)
            sel.append(s)
            scale.append(jnp.sum(s * gsum[j:j + 1], axis=1, keepdims=True))
        sel = jnp.concatenate(sel, axis=0).astype(BF)
        scale = jnp.concatenate(scale, axis=0)
        scale = jnp.where(first, jnp.ones_like(scale), scale)
        for t in range(0, width, 512):
            got = dot(sel, ag[home, :, t:t + 512], 1, 0) * scale
            stage[r % SLOTS, :, :, t:t + 512] = got.astype(BF).reshape(4, CAP, 512)

    def pair_copy(q):
        return remote(psend.at[q % 2], precv.at[q], p_s.at[q], p_r.at[q], partner)

    def back_copy(r):
        dy, dz = offset(r)
        return remote(precv.at[r // 2, r % 2], back.at[r], b_s.at[r], b_r.at[r], (chip(dy, dz), x, c))

    def last_copy(i, d):
        dy, dz = ORDER[EARLY + i]
        return remote(precv.at[7, i, (x + d) % 4], last.at[i, x], l_s.at[i, d], l_r.at[i, d],
                      (chip(dy, dz), (x + d) % 4, c))

    def last_landed(i, d):
        return remote(precv.at[7, i, 0], last.at[i, (x - d + 4) % 4], l_s.at[i, d], l_r.at[i, d], partner)

    def chunk(q):
        for i in range(2):
            forward(q * 2 + i, 1 - c).wait_recv()

        @pl.when(q == 0)
        def _():
            for cp in weights():
                cp.wait()

        gu[...] = dot(rows[0, pl.ds(q * 2, 2)].reshape(256, width), wgu[...], 1, 0)
        hg[...] = dot(rows[1, pl.ds(q * 2, 2)].reshape(256, width), wd[...], 1, 1)

        def act(i, carry):
            at = pl.multiple_of(i * 128, 128)
            to = pl.multiple_of(q * 256 + i * 128, 128)
            for t in range(0, hidden, 128):
                g = gu[pl.ds(at, 128), t:t + 128]
                u = gu[pl.ds(at, 128), hidden + t:hidden + t + 128]
                h = hg[pl.ds(at, 128), t:t + 128]
                s = jax.nn.sigmoid(g)
                a = g * s
                hid[pl.ds(to, 128), t:t + 128] = (a * u).astype(BF)
                grads[pl.ds(to, 128), t:t + 128] = (h * u * s * (1.0 + g * (1.0 - s))).astype(BF)
                grads[pl.ds(to, 128), hidden + t:hidden + t + 128] = (h * a).astype(BF)
            return carry

        lax.fori_loop(0, 2, act, 0)

        @pl.when(q >= 2)
        def _():
            pair_copy(q - 2).wait_send()

        mine = grads[pl.ds(pl.multiple_of(q * 256, 256), 256), :]
        for t in range(0, half, 512):
            w = wgu[pl.ds(pl.multiple_of((1 - c) * half + t, 512), 512), :]
            psend[q % 2, :, :, :, t:t + 512] = dot(mine, w, 1, 1).astype(BF).reshape(2, 4, CAP, 512)
        pair_copy(q).start()
        for t in range(0, half, 512):
            w = wgu[pl.ds(pl.multiple_of(c * half + t, 512), 512), :]
            own[:, t:t + 512] = dot(mine, w, 1, 1)
        pair_copy(q).wait_recv()
        for i in range(2):
            for t in range(0, half, 512):
                both = own[i * 128:(i + 1) * 128, t:t + 512].reshape(4, CAP, 512) + precv[q, i, :, :, t:t + 512].astype(F32)
                precv[q, i, :, :, t:t + 512] = both.astype(BF)
        for i in range(2):
            @pl.when((q < 7) & (q + i > 0))
            def _():
                back_copy(q * 2 + i).start()

        @pl.when(q == 0)
        def _():
            back[0] = precv[0, 0]

        @pl.when(q == 7)
        def _():
            for d in (2, 1, 3, 0):
                for i in range(2):
                    last_copy(i, d).start()

    def finish(r):
        for d in (1, 2, 3):
            x_landed(r, d).wait_recv()
        forward(r, c).start()

    def produce(r):
        dy, dz = offset(r)

        def spread(d, base):
            ay, az = axis_a(d)
            wait_block(ay, az)
            at = chip(ay, az)
            for i, far in enumerate((1, 3, 2)):
                ty, tz = axis_b(far)
                for cp in block_copies(ag.at[at], mag.at[at], ay, az, ty, tz, base + i):
                    cp.start()

        @pl.when(r == 1)
        def _():
            spread(1, 6)
            spread(3, 9)

        @pl.when(r == 3)
        def _():
            spread(2, 12)

        @pl.when(jnp.where(first, dy, dz) != 0)
        def _():
            wait_block(dy, dz)

        @pl.when(r >= SLOTS)
        def _():
            for d in (1, 2, 3):
                x_copy(r - SLOTS, d).wait_send()

        pick(r, chip(dy, dz))
        for d in (1, 3, 2):
            x_copy(r, d).start()
        rows[c, r, x] = stage[r % SLOTS, x]

    def combine(k, t):
        return dot(place[k], back[:, pl.ds(k, 1), :, t:t + 512].reshape(EARLY * CAP, 512), 0, 0)

    def sum_copy(d):
        return remote(xsend.at[d - 1], xrecv.at[d - 1], t_s.at[d - 1], t_r.at[d - 1], (e, (x + d) % 4, c))

    def places():
        for d in (1, 2, 3):
            rank_landed(d).wait_recv()
        for r in range(EARLY):
            dy, dz = ORDER[r]
            for k in range(4):
                m = xrank[k, pl.ds(chip(-dy, -dz), 1), :]
                place[k, r * CAP:(r + 1) * CAP, :] = jnp.where(slot_ids == m, 1.0, 0.0).astype(BF)
        for i in range(2):
            dy, dz = ORDER[EARLY + i]
            for k in range(4):
                m = rank_ref[k, pl.ds(chip(-dy, -dz), 1), :]
                lplace[(i * 4 + k) * CAP:(i * 4 + k + 1) * CAP, :] = jnp.where(slot_ids == m, 1.0, 0.0).astype(BF)

    def early_sums():
        def waits(r, carry):
            back_copy(r).wait_recv()
            return carry

        lax.fori_loop(1, EARLY, waits, 0)
        for d in (2, 1, 3):
            for t in range(0, half, 512):
                xsend[d - 1, :, t:t + 512] = combine((x + d) % 4, t).astype(BF)
            sum_copy(d).start()

    def step(s, carry):
        @pl.when(s < 16)
        def _():
            produce(s)

        @pl.when((s >= LAG) & (s < 16 + LAG))
        def _():
            finish(s - LAG)

        @pl.when(s == 9)
        def _():
            places()

        @pl.when(s == 16 + LAG)
        def _():
            early_sums()

        @pl.when((s > LAG) & ((s - LAG) % 2 == 0))
        def _():
            chunk((s - LAG) // 2 - 1)
        return carry

    lax.fori_loop(0, 17 + LAG, step, 0)

    def grad_out(t):
        at = pl.ds(pl.multiple_of(t * 512, 512), 512)
        return (pltpu.make_async_copy(gtile.at[t % 2, :, pl.ds(0, hidden)], og_ref.at[0, at, :], og_s.at[0, t]),
                pltpu.make_async_copy(gtile.at[t % 2, :, pl.ds(hidden, hidden)], ou_ref.at[0, at, :], og_s.at[1, t]),
                pltpu.make_async_copy(dtile.at[t % 2], od_ref.at[0, :, at], od_s.at[t]))

    for t in range(4):
        cols = slice(t * 512, (t + 1) * 512)
        if t >= 2:
            for cp in grad_out(t - 2):
                cp.wait()
        gtile[t % 2] = dot(rows[0, :, :, :, cols].reshape(2048, 512), grads[...], 0, 0).astype(BF)
        dtile[t % 2] = dot(hid[...], rows[1, :, :, :, cols].reshape(2048, 512), 0, 0).astype(BF)
        for cp in grad_out(t):
            cp.start()

    for t in range(0, half, 512):
        own[0:128, t:t + 512] = combine(x, t)
    for d in (1, 3, 2):
        sum_copy(d).wait_recv()
        own[0:128, :] = own[0:128, :] + xrecv[d - 1].astype(F32)
    for i in range(2):
        for d in range(4):
            last_landed(i, d).wait_recv()
    for t in range(0, half, 512):
        got = dot(lplace[...], last[:, :, :, t:t + 512].reshape(8 * CAP, 512), 0, 0)
        tok_ref[:, t:t + 512] = (own[0:128, t:t + 512] + got).astype(BF)

    def close(r, carry):
        forward(r, c).wait_send()

        @pl.when(r >= 16 - SLOTS)
        def _():
            for d in (1, 2, 3):
                x_copy(r, d).wait_send()

        @pl.when((r >= 1) & (r < EARLY))
        def _():
            back_copy(r).wait_send()
        return carry

    lax.fori_loop(0, 16, close, 0)
    for i in range(2):
        for d in range(4):
            last_copy(i, d).wait_send()
    for slot in range(15):
        for cp in block_copies(ag.at[e], meta_ref, 0, 0, 0, 1, slot):
            cp.wait_send()
    for d in (1, 2, 3):
        rank_copy(d).wait_send()
        sum_copy(d).wait_send()
    for q in (6, 7):
        pair_copy(q).wait_send()
    for t in (2, 3):
        for cp in grad_out(t):
            cp.wait()


def layer(tokens, cotangent, meta, ranks, w_gate, w_up, w_down):
    width = tokens.shape[1]
    hidden = w_gate.shape[2]
    half = width // 2
    dma = pltpu.SemaphoreType.DMA
    vmem = pl.BlockSpec(memory_space=pltpu.VMEM)
    hbm = pl.BlockSpec(memory_space=pl.ANY)
    return pl.pallas_call(
        layer_kernel,
        out_shape=(
            jax.ShapeDtypeStruct((128, half), BF),
            jax.ShapeDtypeStruct((1, width, hidden), BF),
            jax.ShapeDtypeStruct((1, width, hidden), BF),
            jax.ShapeDtypeStruct((1, hidden, width), BF),
        ),
        in_specs=[hbm, hbm, vmem, vmem, hbm, hbm, hbm],
        out_specs=(vmem, hbm, hbm, hbm),
        scratch_shapes=[
            pltpu.VMEM((16, 128, width), BF),
            pltpu.VMEM((16, 16, 16, 128), BF),
            pltpu.VMEM((SLOTS, 4, CAP, width), BF),
            pltpu.VMEM((2, 16, 4, CAP, width), BF),
            pltpu.VMEM((width, 2 * hidden), BF),
            pltpu.VMEM((hidden, width), BF),
            pltpu.VMEM((2048, hidden), BF),
            pltpu.VMEM((2048, 2 * hidden), BF),
            pltpu.VMEM((256, 2 * hidden), F32),
            pltpu.VMEM((256, hidden), F32),
            pltpu.VMEM((2, 2, 4, CAP, half), BF),
            pltpu.VMEM((8, 2, 4, CAP, half), BF),
            pltpu.VMEM((256, half), F32),
            pltpu.VMEM((EARLY, 4, CAP, half), BF),
            pltpu.VMEM((2, 4, CAP, half), BF),
            pltpu.VMEM((4, 16, 128), F32),
            pltpu.VMEM((4, EARLY * CAP, 128), BF),
            pltpu.VMEM((8 * CAP, 128), BF),
            pltpu.VMEM((3, 128, half), BF),
            pltpu.VMEM((3, 128, half), BF),
            pltpu.VMEM((2, 512, 2 * hidden), BF),
            pltpu.VMEM((2, hidden, 512), BF),
            dma((15,)), dma((16,)), dma((15,)), dma((16,)), dma((48,)), dma((48,)), dma((16,)), dma((16,)),
            dma((8,)), dma((8,)), dma((EARLY,)), dma((EARLY,)), dma((2, 4)), dma((2, 4)),
            dma((3,)), dma((3,)), dma((3,)), dma((3,)), dma((3,)), dma((2, 4)), dma((4,)), pltpu.SemaphoreType.DMA,
        ],
        compiler_params=pltpu.CompilerParams(collective_id=0, has_side_effects=True, vmem_limit_bytes=67043328),
    )(tokens, cotangent, meta, ranks, w_gate, w_up, w_down)


def routing(routes, gates):
    ids = jnp.arange(64, dtype=jnp.int32)
    hit = ids[:, None, None] == routes.T[None]
    mask = jnp.sum(hit.astype(F32), axis=1)
    gmap = jnp.sum(jnp.where(hit, gates.T[None], 0.0), axis=1)
    before = jnp.triu(jnp.ones((128, 128), BF), 1)
    rank = jnp.dot(mask.astype(BF), before, preferred_element_type=F32)
    rank = jnp.where(mask > 0, rank, 64.0)
    high = lax.reduce_precision(gmap, 8, 7)
    rest = gmap - high
    mid = lax.reduce_precision(rest, 8, 7)
    low = rest - mid
    return rank, jnp.stack([rank, high, mid, low]).astype(BF)


def body(tokens, cotangent, routes, gates, gate_weight, up_weight, down_weight):
    rank, maps = routing(routes, gates)
    meta = maps.reshape(4, 16, 4, 128).transpose(1, 0, 2, 3).reshape(16, 16, 128)
    ranks = rank.reshape(16, 4, 128).transpose(1, 0, 2)
    return layer(tokens, cotangent, meta, ranks, gate_weight, up_weight, down_weight)


def solution(mesh):
    in_specs = (
        P(("expert", "replica"), None),
        P(("expert", "replica"), None),
        P(("expert", "replica"), None),
        P(("expert", "replica"), None),
        P("expert", None, "tensor"),
        P("expert", None, "tensor"),
        P("expert", "tensor", None),
    )
    out_specs = (
        P(("expert", "replica"), "tensor"),
        P(("expert", "replica"), None, "tensor"),
        P(("expert", "replica"), None, "tensor"),
        P(("expert", "replica"), "tensor", None),
    )
    return jax.shard_map(body, mesh=mesh, in_specs=in_specs, out_specs=out_specs, check_vma=False)
```

time: 203 us -> 179 us (0.88)
  Pallas kernels: 189 us -> 169 us
    pallas_call x1, Pallas kernels: 189 us -> 169 us  [layer(): pl.pallas_call(layer_kernel, out_shape=(jax.ShapeDtypeStruct((128, half),...]
where the time goes in v3:
time: 179 us
  Pallas kernels  169 us (94%)
  local copies, waits for them, and re-layouts  8.9 us (5%)
    pallas_call x1, Pallas kernels, layer(): pl.pallas_call(layer_kernel, out_shape=(jax.ShapeDtypeStruct((128, half),...  169 us
    unnamed x8, local copies, waits for them, and re-layouts  7.62 us

profile of v3, /device:TPU:11, one launch (start us, length us, event | category | flops | bytes accessed | tf_op | source)
XLA Modules:
  0.0 179.2 jit_solution(713390543016845179)
XLA Ops:
  0.6 0.9 convert_reduce_fusion
  1.5 0.1 fusion.8
  1.7 0.7 copy.23
  2.3 0.6 copy.32
  3.0 168.6 %shard_map.102 = (bf16[128,1024]{1,0:T(8,128)(2,1)}, bf16[1,2048,384]{2,1,0:T(8,128)(2,1)}, bf16[1,2048,384]{2,1,0:T(8,128)(2,1)}, bf16[1,384,2048]{2,1,0:T(8,128)(2,1)}) custom-call(bf16[128,2048]{1,0:T(8,128)(2,1)} %token_ref.1, bf16[128,2048]{1,0:T(8,128)(2,1)} %cot_ref.1, bf16[16,16,128]{2,1,0:T(8,128)(2,1)} %bitcast.11, f32[4,16,128]{2,1,0:T(8,128)} %bitcast.12, ...), custom_call_target="tpu_custom_call" | custom-call | tf_op jit(solution)/shard_map/pallas_call | solution.py:386
  171.5 1.7 copy.37
  173.2 0.0 copy-start.1
  173.2 2.8 %copy.38 = bf16[1,2048,384]{2,1,0:T(8,128)(2,1)} copy(bf16[1,2048,384]{2,1,0:T(8,128)(2,1)} %get-tuple-element.16) | data formatting | bytes 3145728
  176.0 0.0 copy-done.1
  176.0 0.0 copy-start
  176.0 1.1 copy.39
  177.2 0.8 copy-done
  178.0 1.1 copy.40
  (3 shorter events, 0.0 us)
Async XLA Ops:
  173.2 2.8 %copy-start.1 = (bf16[1,2048,384]{2,1,0:T(8,128)(2,1)S(1)}, bf16[1,2048,384]{2,1,0:T(8,128)(2,1)}, u32[]{:S(2)}) copy-start(bf16[1,2048,384]{2,1,0:T(8,128)(2,1)} %get-tuple-element.17) | copy-start | bytes 4718596
  176.0 2.0 %copy-start = (bf16[1,384,2048]{2,1,0:T(8,128)(2,1)S(1)}, bf16[1,384,2048]{2,1,0:T(8,128)(2,1)}, u32[]{:S(2)}) copy-start(bf16[1,384,2048]{2,1,0:T(8,128)(2,1)} %get-tuple-element.18) | copy-start | bytes 4718596

commit v4 on v3

--- a/solution.py
+++ b/solution.py
@@ -55,11 +55,8 @@
         return pltpu.make_async_remote_copy(src_ref=src, dst_ref=dst, send_sem=send, recv_sem=recv,
                                             device_id=dev, device_id_type=MESH)
 
-    def axis_a(d):
-        return jnp.where(first, 0, d), jnp.where(first, d, 0)
-
-    def axis_b(d):
-        return jnp.where(first, d, 0), jnp.where(first, 0, d)
+    def at(a, b):
+        return jnp.where(first, b, a), jnp.where(first, a, b)
 
     partner = (e, x, 1 - c)
 
@@ -89,23 +86,73 @@
     pltpu.make_async_copy(token_ref, ag.at[e], i_s).wait()
     pl.semaphore_wait(barrier, 31)
 
-    def block_copies(src, msrc, by, bz, ty, tz, slot):
+    def meta_copy(rel):
+        dy, dz = rel // 4, rel % 4
+        target = chip(dy, dz)
+        landed = ((4 - dy) % 4) * 4 + (4 - dz) % 4
+        return remote(meta_ref.at[target], mag.at[e], mg_s.at[rel], mg_r.at[landed], (target, x, c))
+
+    def block_copy(a, b, da, db, slot, part=None):
+        by, bz = at(a, b)
+        ty, tz = at(da, db)
         home = chip(by, bz)
         landed = ((by - ty + 4) % 4) * 4 + (bz - tz + 4) % 4
-        dev = (chip(ty, tz), x, c)
-        return (remote(msrc, mag.at[home], mg_s.at[slot], mg_r.at[landed], dev),
-                remote(src, ag.at[home], ag_s.at[slot], ag_r.at[landed], dev))
-
-    def wait_block(by, bz):
+        if part is None:
+            piece, recv = ag.at[home], ag_r.at[landed, 0]
+        else:
+            piece, recv = ag.at[home, pl.ds(part * 64, 64)], ag_r.at[landed, part]
+        return remote(piece, piece, ag_s.at[slot], recv, (chip(ty, tz), x, c))
+
+    def wait_block(a, b, parts=False):
+        by, bz = at(a, b)
         rel, home = by * 4 + bz, chip(by, bz)
-        remote(meta_ref, mag.at[home], mg_s.at[0], mg_r.at[rel], partner).wait_recv()
-        remote(ag.at[e], ag.at[home], ag_s.at[0], ag_r.at[rel], partner).wait_recv()
-
-    for i, d in enumerate((1, 3, 2)):
-        for ax, base in ((axis_a, 0), (axis_b, 3)):
-            ty, tz = ax(d)
-            for cp in block_copies(ag.at[e], meta_ref, 0, 0, ty, tz, base + i):
-                cp.start()
+        if parts:
+            for part in range(2):
+                piece = ag.at[home, pl.ds(part * 64, 64)]
+                remote(piece, piece, ag_s.at[0], ag_r.at[rel, part], partner).wait_recv()
+        else:
+            remote(ag.at[home], ag.at[home], ag_s.at[0], ag_r.at[rel, 0], partner).wait_recv()
+
+    def relay(a, slot):
+        wait_block(a, 1)
+        block_copy(a, 1, 0, 3, slot, 0).start()
+        wait_block(a, 3)
+        block_copy(a, 3, 0, 1, slot + 1, 1).start()
+
+    def gather(s):
+        @pl.when(s == 1)
+        def _():
+            wait_block(1, 0)
+            block_copy(1, 0, 3, 0, 4, 0).start()
+            wait_block(3, 0)
+            block_copy(3, 0, 1, 0, 5, 1).start()
+            block_copy(1, 0, 0, 1, 6).start()
+            block_copy(1, 0, 0, 3, 7).start()
+            block_copy(3, 0, 0, 1, 8).start()
+            block_copy(3, 0, 0, 3, 9).start()
+            relay(0, 12)
+            for rel in range(1, 16):
+                meta_copy(rel).wait_recv()
+
+        @pl.when(s == 3)
+        def _():
+            wait_block(2, 0, True)
+            block_copy(2, 0, 0, 1, 10).start()
+            block_copy(2, 0, 0, 3, 11).start()
+
+        @pl.when(s == 5)
+        def _():
+            relay(1, 14)
+            relay(3, 16)
+
+        @pl.when(s == 7)
+        def _():
+            relay(2, 18)
+
+    for rel in range(1, 16):
+        meta_copy(rel).start()
+    for i, (da, db) in enumerate(((1, 0), (3, 0), (0, 1), (0, 3))):
+        block_copy(0, 0, da, db, i).start()
 
     def rank_copy(d):
         return remote(rank_ref.at[(x + d) % 4], xrank.at[x], k_s.at[d - 1], k_r.at[d - 1], (e, (x + d) % 4, c))
@@ -116,7 +163,7 @@
     for d in (1, 2, 3):
         rank_copy(d).start()
     xrank[x] = rank_ref[x]
-    mag[e] = meta_ref[...]
+    mag[e] = meta_ref[e]
     for cp in weights():
         cp.start()
 
@@ -134,7 +181,7 @@
     slot_ids = lax.broadcasted_iota(jnp.int32, (CAP, 128), 0).astype(F32)
 
     def pick(r, home):
-        m = mag[home, e].astype(F32)
+        m = mag[home].astype(F32)
         gsum = m[4:8] + m[8:12] + m[12:16]
         sel, scale = [], []
         for j in range(4):
@@ -231,27 +278,9 @@
     def produce(r):
         dy, dz = offset(r)
 
-        def spread(d, base):
-            ay, az = axis_a(d)
-            wait_block(ay, az)
-            at = chip(ay, az)
-            for i, far in enumerate((1, 3, 2)):
-                ty, tz = axis_b(far)
-                for cp in block_copies(ag.at[at], mag.at[at], ay, az, ty, tz, base + i):
-                    cp.start()
-
-        @pl.when(r == 1)
-        def _():
-            spread(1, 6)
-            spread(3, 9)
-
-        @pl.when(r == 3)
-        def _():
-            spread(2, 12)
-
-        @pl.when(jnp.where(first, dy, dz) != 0)
-        def _():
-            wait_block(dy, dz)
+        @pl.when(jnp.where(first, dy, dz) == 2)
+        def _():
+            wait_block(jnp.where(first, dz, dy), 2, True)
 
         @pl.when(r >= SLOTS)
         def _():
@@ -297,6 +326,7 @@
     def step(s, carry):
         @pl.when(s < 16)
         def _():
+            gather(s)
             produce(s)
 
         @pl.when((s >= LAG) & (s < 16 + LAG))
@@ -363,9 +393,11 @@
     for i in range(2):
         for d in range(4):
             last_copy(i, d).wait_send()
-    for slot in range(15):
-        for cp in block_copies(ag.at[e], meta_ref, 0, 0, 0, 1, slot):
-            cp.wait_send()
+    for slot in range(20):
+        half_sent = slot in (4, 5) or slot >= 12
+        block_copy(0, 0, 1, 0, slot, 0 if half_sent else None).wait_send()
+    for rel in range(1, 16):
+        meta_copy(rel).wait_send()
     for d in (1, 2, 3):
         rank_copy(d).wait_send()
         sum_copy(d).wait_send()
@@ -395,7 +427,7 @@
         out_specs=(vmem, hbm, hbm, hbm),
         scratch_shapes=[
             pltpu.VMEM((16, 128, width), BF),
-            pltpu.VMEM((16, 16, 16, 128), BF),
+            pltpu.VMEM((16, 16, 128), BF),
             pltpu.VMEM((SLOTS, 4, CAP, width), BF),
             pltpu.VMEM((2, 16, 4, CAP, width), BF),
             pltpu.VMEM((width, 2 * hidden), BF),
@@ -416,7 +448,7 @@
             pltpu.VMEM((3, 128, half), BF),
             pltpu.VMEM((2, 512, 2 * hidden), BF),
             pltpu.VMEM((2, hidden, 512), BF),
-            dma((15,)), dma((16,)), dma((15,)), dma((16,)), dma((48,)), dma((48,)), dma((16,)), dma((16,)),
+            dma((20,)), dma((16, 2)), dma((16,)), dma((16,)), dma((48,)), dma((48,)), dma((16,)), dma((16,)),
             dma((8,)), dma((8,)), dma((EARLY,)), dma((EARLY,)), dma((2, 4)), dma((2, 4)),
             dma((3,)), dma((3,)), dma((3,)), dma((3,)), dma((3,)), dma((2, 4)), dma((4,)), pltpu.SemaphoreType.DMA,
         ],

time: 179 us -> 161 us (0.90)
  the two profiles are of different devices: /device:TPU:11 before, /device:TPU:1 now
where the time goes in v4:
time: 161 us; the launch traced here: 160 us
  Pallas kernels  150 us (93%)
  local copies, waits for them, and re-layouts  8.9 us (6%)
    pallas_call x1, Pallas kernels, layer(): pl.pallas_call(layer_kernel, out_shape=(jax.ShapeDtypeStruct((128, half),...  150 us
    unnamed x8, local copies, waits for them, and re-layouts  7.62 us

profile of v4, /device:TPU:1, one launch (start us, length us, event | category | flops | bytes accessed | tf_op | source)
XLA Modules:
  0.0 160.4 jit_solution(11605199123656705801)
XLA Ops:
  0.6 0.9 convert_reduce_fusion
  1.5 0.1 fusion.8
  1.7 0.7 copy.23
  2.3 0.6 copy.32
  3.0 149.9 %shard_map.102 = (bf16[128,1024]{1,0:T(8,128)(2,1)}, bf16[1,2048,384]{2,1,0:T(8,128)(2,1)}, bf16[1,2048,384]{2,1,0:T(8,128)(2,1)}, bf16[1,384,2048]{2,1,0:T(8,128)(2,1)}) custom-call(bf16[128,2048]{1,0:T(8,128)(2,1)} %token_ref.1, bf16[128,2048]{1,0:T(8,128)(2,1)} %cot_ref.1, bf16[16,16,128]{2,1,0:T(8,128)(2,1)} %bitcast.11, f32[4,16,128]{2,1,0:T(8,128)} %bitcast.12, ...), custom_call_target="tpu_custom_call" | custom-call | tf_op jit(solution)/shard_map/pallas_call | solution.py:418
  152.8 1.7 %copy.37 = bf16[128,1024]{1,0:T(8,128)(2,1)} copy(bf16[128,1024]{1,0:T(8,128)(2,1)} %get-tuple-element.15) | data formatting | bytes 524288
  154.5 0.0 copy-start.1
  154.5 2.8 %copy.38 = bf16[1,2048,384]{2,1,0:T(8,128)(2,1)} copy(bf16[1,2048,384]{2,1,0:T(8,128)(2,1)} %get-tuple-element.16) | data formatting | bytes 3145728
  157.3 0.0 copy-done.1
  157.3 0.0 copy-start
  157.3 1.1 copy.39
  158.5 0.8 copy-done
  159.3 1.1 copy.40
  (3 shorter events, 0.0 us)
Async XLA Ops:
  154.5 2.8 %copy-start.1 = (bf16[1,2048,384]{2,1,0:T(8,128)(2,1)S(1)}, bf16[1,2048,384]{2,1,0:T(8,128)(2,1)}, u32[]{:S(2)}) copy-start(bf16[1,2048,384]{2,1,0:T(8,128)(2,1)} %get-tuple-element.17) | copy-start | bytes 4718596
  157.3 2.0 %copy-start = (bf16[1,384,2048]{2,1,0:T(8,128)(2,1)S(1)}, bf16[1,384,2048]{2,1,0:T(8,128)(2,1)}, u32[]{:S(2)}) copy-start(bf16[1,384,2048]{2,1,0:T(8,128)(2,1)} %get-tuple-element.18) | copy-start | bytes 4718596

commit v5 on v4

--- a/solution.py
+++ b/solution.py
@@ -37,7 +37,7 @@
 def layer_kernel(token_ref, cot_ref, meta_ref, rank_ref, wg_ref, wu_ref, wd_ref,
                  tok_ref, og_ref, ou_ref, od_ref,
                  ag, mag, stage, rows, wgu, wd, hid, grads, gu, hg, psend, precv, own, back,
-                 last, xrank, place, lplace, xsend, xrecv, gtile, dtile,
+                 last, xrank, place, lplace, xsend, xrecv, gacc, dacc, gtile, dtile,
                  ag_s, ag_r, mg_s, mg_r, x_s, x_r, f_s, f_r, p_s, p_r, b_s, b_r, l_s, l_r, k_s, k_r, t_s, t_r, w_s, og_s, od_s, i_s):
     e = lax.axis_index("expert")
     x = lax.axis_index("replica")
@@ -323,6 +323,22 @@
                 xsend[d - 1, :, t:t + 512] = combine((x + d) % 4, t).astype(BF)
             sum_copy(d).start()
 
+    def grad_part(k, cols):
+        span = pl.ds(pl.multiple_of(k * 512, 512), 512)
+        blocks = pl.ds(k * 4, 4)
+        return (dot(rows[0, blocks, :, :, cols].reshape(512, 512), grads[span, :], 0, 0),
+                dot(hid[span, :], rows[1, blocks, :, :, cols].reshape(512, 512), 0, 0))
+
+    def accumulate(k):
+        for t in range(4):
+            cols = slice(t * 512, (t + 1) * 512)
+            more_g, more_d = grad_part(k, cols)
+            gacc[cols, :] = gacc[cols, :] + more_g
+            dacc[:, cols] = dacc[:, cols] + more_d
+
+    gacc[...] = jnp.zeros_like(gacc)
+    dacc[...] = jnp.zeros_like(dacc)
+
     def step(s, carry):
         @pl.when(s < 16)
         def _():
@@ -337,16 +353,17 @@
         def _():
             places()
 
-        @pl.when(s == 16 + LAG)
-        def _():
-            early_sums()
-
         @pl.when((s > LAG) & ((s - LAG) % 2 == 0))
         def _():
             chunk((s - LAG) // 2 - 1)
+
+        @pl.when((s > LAG) & (s < 16 + LAG) & ((s - LAG) % 4 == 0))
+        def _():
+            accumulate((s - LAG) // 4 - 1)
         return carry
 
     lax.fori_loop(0, 17 + LAG, step, 0)
+    early_sums()
 
     def grad_out(t):
         at = pl.ds(pl.multiple_of(t * 512, 512), 512)
@@ -359,8 +376,9 @@
         if t >= 2:
             for cp in grad_out(t - 2):
                 cp.wait()
-        gtile[t % 2] = dot(rows[0, :, :, :, cols].reshape(2048, 512), grads[...], 0, 0).astype(BF)
-        dtile[t % 2] = dot(hid[...], rows[1, :, :, :, cols].reshape(2048, 512), 0, 0).astype(BF)
+        more_g, more_d = grad_part(3, cols)
+        gtile[t % 2] = (gacc[cols, :] + more_g).astype(BF)
+        dtile[t % 2] = (dacc[:, cols] + more_d).astype(BF)
         for cp in grad_out(t):
             cp.start()
 
@@ -446,6 +464,8 @@
             pltpu.VMEM((8 * CAP, 128), BF),
             pltpu.VMEM((3, 128, half), BF),
             pltpu.VMEM((3, 128, half), BF),
+            pltpu.VMEM((width, 2 * hidden), F32),
+            pltpu.VMEM((hidden, width), F32),
             pltpu.VMEM((2, 512, 2 * hidden), BF),
             pltpu.VMEM((2, hidden, 512), BF),
             dma((20,)), dma((16, 2)), dma((16,)), dma((16,)), dma((48,)), dma((48,)), dma((16,)), dma((16,)),

time: 161 us -> 155 us (0.963)
  the two profiles are of different devices: /device:TPU:1 before, /device:TPU:11 now
where the time goes in v5:
time: 155 us; the launch traced here: 152 us
  Pallas kernels  141 us (91%)
  local copies, waits for them, and re-layouts  8.9 us (6%)
    pallas_call x1, Pallas kernels, layer(): pl.pallas_call(layer_kernel, out_shape=(jax.ShapeDtypeStruct((128, half),...  141 us
    unnamed x8, local copies, waits for them, and re-layouts  7.62 us

profile of v5, /device:TPU:11, one launch (start us, length us, event | category | flops | bytes accessed | tf_op | source)
XLA Modules:
  0.0 151.5 jit_solution(8027131464588999197)
XLA Ops:
  0.6 0.9 convert_reduce_fusion
  1.5 0.1 fusion.8
  1.7 0.7 copy.23
  2.3 0.6 copy.32
  3.0 140.9 %shard_map.102 = (bf16[128,1024]{1,0:T(8,128)(2,1)}, bf16[1,2048,384]{2,1,0:T(8,128)(2,1)}, bf16[1,2048,384]{2,1,0:T(8,128)(2,1)}, bf16[1,384,2048]{2,1,0:T(8,128)(2,1)}) custom-call(bf16[128,2048]{1,0:T(8,128)(2,1)} %token_ref.1, bf16[128,2048]{1,0:T(8,128)(2,1)} %cot_ref.1, bf16[16,16,128]{2,1,0:T(8,128)(2,1)} %bitcast.11, f32[4,16,128]{2,1,0:T(8,128)} %bitcast.12, ...), custom_call_target="tpu_custom_call" | custom-call | tf_op jit(solution)/shard_map/pallas_call | solution.py:436
  143.9 1.7 %copy.37 = bf16[128,1024]{1,0:T(8,128)(2,1)} copy(bf16[128,1024]{1,0:T(8,128)(2,1)} %get-tuple-element.15) | data formatting | bytes 524288
  145.6 0.0 copy-start.1
  145.6 2.8 %copy.38 = bf16[1,2048,384]{2,1,0:T(8,128)(2,1)} copy(bf16[1,2048,384]{2,1,0:T(8,128)(2,1)} %get-tuple-element.16) | data formatting | bytes 3145728
  148.4 0.0 copy-done.1
  148.4 0.0 copy-start
  148.4 1.1 copy.39
  149.6 0.8 copy-done
  150.4 1.1 copy.40
  (3 shorter events, 0.0 us)
Async XLA Ops:
  145.6 2.8 %copy-start.1 = (bf16[1,2048,384]{2,1,0:T(8,128)(2,1)S(1)}, bf16[1,2048,384]{2,1,0:T(8,128)(2,1)}, u32[]{:S(2)}) copy-start(bf16[1,2048,384]{2,1,0:T(8,128)(2,1)} %get-tuple-element.17) | copy-start | bytes 4718596
  148.4 2.0 %copy-start = (bf16[1,384,2048]{2,1,0:T(8,128)(2,1)S(1)}, bf16[1,384,2048]{2,1,0:T(8,128)(2,1)}, u32[]{:S(2)}) copy-start(bf16[1,384,2048]{2,1,0:T(8,128)(2,1)} %get-tuple-element.18) | copy-start | bytes 4718596

commit v6 on v5

--- a/solution.py
+++ b/solution.py
@@ -14,6 +14,7 @@
 ORDER = ((0, 0), (0, 1), (1, 0), (0, 2), (2, 0), (1, 1), (3, 3), (2, 1),
          (1, 2), (3, 2), (2, 3), (2, 2), (1, 3), (3, 1), (0, 3), (3, 0))
 EARLY = 14
+MIRRORED = (1, 3, 7, 9, 12, 14)
 
 
 def entry(r, column):
@@ -126,13 +127,18 @@
             block_copy(1, 0, 3, 0, 4, 0).start()
             wait_block(3, 0)
             block_copy(3, 0, 1, 0, 5, 1).start()
+            block_copy(0, 0, 0, 1, 2).start()
+            block_copy(0, 0, 0, 3, 3).start()
             block_copy(1, 0, 0, 1, 6).start()
             block_copy(1, 0, 0, 3, 7).start()
             block_copy(3, 0, 0, 1, 8).start()
             block_copy(3, 0, 0, 3, 9).start()
-            relay(0, 12)
             for rel in range(1, 16):
                 meta_copy(rel).wait_recv()
+
+        @pl.when(s == 2)
+        def _():
+            relay(0, 12)
 
         @pl.when(s == 3)
         def _():
@@ -151,8 +157,8 @@
 
     for rel in range(1, 16):
         meta_copy(rel).start()
-    for i, (da, db) in enumerate(((1, 0), (3, 0), (0, 1), (0, 3))):
-        block_copy(0, 0, da, db, i).start()
+    block_copy(0, 0, 1, 0, 0).start()
+    block_copy(0, 0, 3, 0, 1).start()
 
     def rank_copy(d):
         return remote(rank_ref.at[(x + d) % 4], xrank.at[x], k_s.at[d - 1], k_r.at[d - 1], (e, (x + d) % 4, c))
@@ -339,15 +345,21 @@
     gacc[...] = jnp.zeros_like(gacc)
     dacc[...] = jnp.zeros_like(dacc)
 
+    def turn(s):
+        swap = 0
+        for k in MIRRORED:
+            swap = swap + jnp.where(s == k, 1, 0) - jnp.where(s == k + 1, 1, 0)
+        return jnp.where(first, s, s + swap)
+
     def step(s, carry):
         @pl.when(s < 16)
         def _():
             gather(s)
-            produce(s)
+            produce(turn(s))
 
         @pl.when((s >= LAG) & (s < 16 + LAG))
         def _():
-            finish(s - LAG)
+            finish(turn(s - LAG))
 
         @pl.when(s == 9)
         def _():

time: 155 us -> 153 us (0.987)
  no operation moved by 1% of the time
where the time goes in v6:
time: 153 us; the launch traced here: 150 us
  Pallas kernels  140 us (92%)
  local copies, waits for them, and re-layouts  8.9 us (6%)
    pallas_call x1, Pallas kernels, layer(): pl.pallas_call(layer_kernel, out_shape=(jax.ShapeDtypeStruct((128, half),...  140 us
    unnamed x8, local copies, waits for them, and re-layouts  7.62 us

profile of v6, /device:TPU:11, one launch (start us, length us, event | category | flops | bytes accessed | tf_op | source)
XLA Modules:
  0.0 150.3 jit_solution(12906576512625893535)
XLA Ops:
  0.6 0.9 convert_reduce_fusion
  1.5 0.1 fusion.8
  1.7 0.7 copy.23
  2.3 0.6 copy.32
  3.0 139.7 %shard_map.102 = (bf16[128,1024]{1,0:T(8,128)(2,1)}, bf16[1,2048,384]{2,1,0:T(8,128)(2,1)}, bf16[1,2048,384]{2,1,0:T(8,128)(2,1)}, bf16[1,384,2048]{2,1,0:T(8,128)(2,1)}) custom-call(bf16[128,2048]{1,0:T(8,128)(2,1)} %token_ref.1, bf16[128,2048]{1,0:T(8,128)(2,1)} %cot_ref.1, bf16[16,16,128]{2,1,0:T(8,128)(2,1)} %bitcast.11, f32[4,16,128]{2,1,0:T(8,128)} %bitcast.12, ...), custom_call_target="tpu_custom_call" | custom-call | tf_op jit(solution)/shard_map/pallas_call | solution.py:448
  142.7 1.7 %copy.37 = bf16[128,1024]{1,0:T(8,128)(2,1)} copy(bf16[128,1024]{1,0:T(8,128)(2,1)} %get-tuple-element.15) | data formatting | bytes 524288
  144.4 0.0 copy-start.1
  144.4 2.8 %copy.38 = bf16[1,2048,384]{2,1,0:T(8,128)(2,1)} copy(bf16[1,2048,384]{2,1,0:T(8,128)(2,1)} %get-tuple-element.16) | data formatting | bytes 3145728
  147.2 0.0 copy-done.1
  147.2 0.0 copy-start
  147.2 1.1 copy.39
  148.3 0.8 copy-done
  149.2 1.1 copy.40
  (3 shorter events, 0.0 us)
Async XLA Ops:
  144.4 2.8 %copy-start.1 = (bf16[1,2048,384]{2,1,0:T(8,128)(2,1)S(1)}, bf16[1,2048,384]{2,1,0:T(8,128)(2,1)}, u32[]{:S(2)}) copy-start(bf16[1,2048,384]{2,1,0:T(8,128)(2,1)} %get-tuple-element.17) | copy-start | bytes 4718596
  147.2 2.0 %copy-start = (bf16[1,384,2048]{2,1,0:T(8,128)(2,1)S(1)}, bf16[1,384,2048]{2,1,0:T(8,128)(2,1)}, u32[]{:S(2)}) copy-start(bf16[1,384,2048]{2,1,0:T(8,128)(2,1)} %get-tuple-element.18) | copy-start | bytes 4718596
